TPU v7x, 1024 devices: a whole 4x8x16 slice. The times are simulated.
1024 devices in a mesh: section: 8 (over y), shard: 128 (over z, x, core).
Axes of the slice: x: 4, y: 8, z: 16, core: 2. Of those that a mesh axis runs over, the one named last changes fastest.
Arguments:
- section_inputs: bfloat16 [8, 2, 384, 16384], P('section', None, None, 'shard'), may hold values from -12 to 12
- top_grad: bfloat16 [2, 384, 16384], P(None, None, 'shard'), may hold values from -6 to 6
- norm_gain: float32 [8, 16384], P('section', 'shard'), may hold values from 0.1 to 1.9
- key_grad: bfloat16 [8, 2, 384, 512], P('section'), may hold values from -18 to 18
- value_grad: bfloat16 [8, 2, 384, 512], P('section'), may hold values from -6 to 6
- key_weight: bfloat16 [8, 512, 16384], P('section', None, 'shard'), may hold values from -0.046875 to 0.046875
- value_weight: bfloat16 [8, 512, 16384], P('section', None, 'shard'), may hold values from -0.046875 to 0.046875
- first_codes: int32 [8, 2, 512, 16384], P('section', None, None, 'shard'), may hold values from 0 to 15
- second_codes: int32 [8, 2, 512, 16384], P('section', None, None, 'shard'), may hold values from 0 to 15
- first_scale: float32 [8, 2, 512, 128], P('section', None, None, 'shard'), may hold values from 1.726335e-05 to 0.00017263349
- second_scale: float32 [8, 2, 512, 128], P('section', None, None, 'shard'), may hold values from 7.4505807e-10 to 7.450581e-09
Outputs:
- direction: float32 [8, 2, 512, 16384], P('section', None, None, 'shard')
- first_ratio: float32 [8, 2, 512, 16384], P('section', None, None, 'shard')
- second_ratio: float32 [8, 2, 512, 16384], P('section', None, None, 'shard')
- leaving: bfloat16 [8, 2, 384, 16384], P('section', None, None, 'shard')
Inputs may be any that keep to these rules, and one draw needn't show every extreme that they name: `first_codes`: codes follow the encoding of the steps.
All inputs are finite; a program needn't handle non-finite values. Where the computation divides by a largest or mean magnitude, that divisor is 1e-20 or more.
Results may differ from a plain program's by a relative error of at most 0.0085.
The roundings to bfloat16 on the way count: a program that leaves them out, or rounds other values in their place, can miss the bound.
Values may be sent and summed in bfloat16 or wider, within the bound.
No kernel may reach another device: no remote copies, remote signals or barrier semaphores. Data moves between devices by JAX's collectives and lax.ppermute only.
A program may use at most 32 MiB of HBM per device.

v0:
```python
import jax
import jax.numpy as jnp
from jax import lax
from jax.sharding import Mesh
from jax.sharding import PartitionSpec as P

D = 16384
QB = 128
STEP = 20
SHARD = ("shard_0", "shard_1", "shard_2")
SECTION_SHARD = ("section", "shard_0", "shard_1", "shard_2")


beta_one = 0.9
beta_two = 0.95
clip_norm = 1.0


def one_axis_at_a_time(x, axes):
    for axis in axes:
        x = lax.psum(x, axis)
    return x


def optimizer(gradients, square_total, first_codes, second_codes, first_scale, second_scale):
    clip_factor = jnp.minimum(1.0, clip_norm / (jnp.sqrt(square_total) + 1e-06))
    clipped = clip_factor * gradients
    sign_part = 1.0 - 2.0 * (first_codes // 8).astype(jnp.float32)
    first_old = (
        jnp.repeat(first_scale, QB, axis=-1)
        * sign_part
        * jnp.exp2(-(first_codes % 8).astype(jnp.float32))
    )
    second_old = jnp.repeat(second_scale, QB, axis=-1) * jnp.exp2(-second_codes.astype(jnp.float32))
    first_new = beta_one * first_old + (1.0 - beta_one) * clipped
    second_new = beta_two * second_old + (1.0 - beta_two) * clipped * clipped
    bias_one = 1.0 - beta_one**STEP
    bias_two = 1.0 - beta_two**STEP
    direction = first_new / bias_one / (jnp.sqrt(second_new / bias_two) + 1e-08)
    blocks = clipped.reshape(clipped.shape[:-1] + (clipped.shape[-1] // QB, QB))
    first_bound = beta_one * first_scale + (1.0 - beta_one) * jnp.max(jnp.abs(blocks), axis=-1)
    second_bound = beta_two * second_scale + (1.0 - beta_two) * jnp.max(blocks * blocks, axis=-1)
    first_ratio = first_new / jnp.repeat(first_bound, QB, axis=-1)
    second_ratio = second_new / jnp.repeat(second_bound, QB, axis=-1)
    return (direction, first_ratio, second_ratio)


def project(left, right):
    return lax.dot_general(
        left, right, (((0,), (0,)), ((), ())), preferred_element_type=jnp.float32
    )


def on_device(
    section_inputs,
    top_grad,
    norm_gain,
    key_grad,
    value_grad,
    key_weight,
    value_weight,
    first_codes,
    second_codes,
    first_scale,
    second_scale,
):
    micro_count = top_grad.shape[0]
    token_count = top_grad.shape[1]
    width_local = top_grad.shape[2]
    row_count = micro_count * token_count
    section_count = lax.axis_size("section")
    is_last = lax.axis_index("section") == section_count - 1
    inputs = section_inputs[0].reshape(row_count, width_local)
    inputs_f = inputs.astype(jnp.float32)
    gain = norm_gain[0]
    keys_rows = key_grad[0].reshape(row_count, key_grad.shape[3])
    values_rows = value_grad[0].reshape(row_count, value_grad.shape[3])
    d_normed = jnp.dot(keys_rows, key_weight[0], preferred_element_type=jnp.float32) + jnp.dot(
        values_rows, value_weight[0], preferred_element_type=jnp.float32
    )
    local_power = jnp.sum(inputs_f * inputs_f, axis=1)
    local_dot = jnp.sum(inputs_f * gain * d_normed, axis=1)
    power, row_dot = (one_axis_at_a_time(local_power, SHARD), one_axis_at_a_time(local_dot, SHARD))
    root = 1.0 / jnp.sqrt(power / D + 1e-05)
    normed = (inputs_f * root[:, None] * gain).astype(jnp.bfloat16)
    input_grad = (
        gain * d_normed * root[:, None] - inputs_f * (root * root * root * row_dot / D)[:, None]
    )
    top_rows = top_grad.reshape(row_count, width_local).astype(jnp.float32)
    base = input_grad + jnp.where(is_last, top_rows, jnp.zeros_like(top_rows))
    block_rows = row_count // section_count
    split_rows = base.reshape(section_count, block_rows, width_local)
    by_section = lax.all_to_all(split_rows, "section", split_axis=0, concat_axis=0, tiled=True)
    suffix = jnp.flip(jnp.cumsum(jnp.flip(by_section, 0), axis=0), 0).astype(jnp.bfloat16)
    returned = lax.all_to_all(suffix, "section", split_axis=0, concat_axis=0, tiled=True)
    leaving_rows = returned.reshape(row_count, width_local)
    leaving = leaving_rows.reshape(1, micro_count, token_count, width_local)
    gradients = jnp.stack([project(keys_rows, normed), project(values_rows, normed)])
    square_total = one_axis_at_a_time(jnp.sum(gradients * gradients), SECTION_SHARD)
    direction, first_ratio, second_ratio = optimizer(
        gradients, square_total, first_codes[0], second_codes[0], first_scale[0], second_scale[0]
    )
    return (direction[None], first_ratio[None], second_ratio[None], leaving)


def solution(mesh):
    finer = Mesh(
        mesh.devices.reshape(mesh.shape["section"], 16, 4, 2),
        ("section", "shard_0", "shard_1", "shard_2"),
    )
    in_specs = (
        P("section", None, None, SHARD),
        P(None, None, SHARD),
        P("section", SHARD),
        P("section", None, None, None),
        P("section", None, None, None),
        P("section", None, SHARD),
        P("section", None, SHARD),
        P("section", None, None, SHARD),
        P("section", None, None, SHARD),
        P("section", None, None, SHARD),
        P("section", None, None, SHARD),
    )
    out_specs = (
        P("section", None, None, SHARD),
        P("section", None, None, SHARD),
        P("section", None, None, SHARD),
        P("section", None, None, SHARD),
    )
    return jax.shard_map(
        on_device, mesh=finer, in_specs=in_specs, out_specs=out_specs, check_vma=False
    )
```

profile of v0, /device:TPU:2, one launch (start us, length us, event | category | flops | bytes accessed | tf_op | source)
XLA Modules:
  0.0 158.2 jit_solution(8922316772827195125)
XLA Ops:
  0.6 0.0 copy-start
  0.7 1.2 fusion.21
  1.9 43.3 %psum.70 = f32[768]{0:T(1024)S(1)} all-reduce(f32[768]{0:T(1024)S(1)} %reduce_sum.30), channel_id=1, replica_groups=mesh['section'=8,'shard_0'=16,'shard_1'=4,'shard_2'=2] {'shard_0'}, use_global_device_ids=true, to_apply=%region_1.0 | all-reduce | flops 768 | bytes 6144 | tf_op jit(solution)/shard_map/psum | solution.py:21
  45.3 8.6 %psum.71 = f32[768]{0:T(1024)S(1)} all-reduce(f32[768]{0:T(1024)S(1)} %psum.70), channel_id=1, replica_groups=mesh['section'=8,'shard_0'=16,'shard_1'=4,'shard_2'=2] {'shard_1'}, use_global_device_ids=true, to_apply=%region_2.0 | all-reduce | flops 768 | bytes 6144 | tf_op jit(solution)/shard_map/psum | solution.py:21
  53.9 2.5 %psum.72 = f32[768]{0:T(1024)S(1)} all-reduce(f32[768]{0:T(1024)S(1)} %psum.71), channel_id=1, replica_groups=mesh['section'=8,'shard_0'=16,'shard_1'=4,'shard_2'=2] {'shard_2'}, use_global_device_ids=true, to_apply=%region_3.0 | all-reduce | flops 768 | bytes 6144 | tf_op jit(solution)/shard_map/psum | solution.py:21
  56.4 1.2 fusion
  57.5 0.4 fusion.2
  58.0 0.7 fusion.16
  58.7 18.2 %psum.73 = f32[]{:T(128)} all-reduce(f32[]{:T(128)} %fusion.16), channel_id=1, replica_groups=mesh['section'=8,'shard_0'=16,'shard_1'=4,'shard_2'=2] {'section'}, use_global_device_ids=true, to_apply=%region_5.0 | all-reduce | flops 1 | bytes 8 | tf_op jit(solution)/shard_map/psum | solution.py:21
  77.0 0.4 fusion.31
  77.3 0.5 copy-done.7
  77.9 0.4 fusion.25
  78.3 28.1 %all-reduce = (f32[]{:T(128)}, f32[768]{0:T(1024)S(1)}) all-reduce(f32[]{:T(128)} %psum.73, f32[768]{0:T(1024)S(1)} %get-tuple-element.20), channel_id=1, replica_groups=mesh['section'=8,'shard_0'=16,'shard_1'=4,'shard_2'=2] {'shard_0'}, use_global_device_ids=true, to_apply=%region_6.0 | all-reduce | flops 769 | bytes 6152 | tf_op jit(solution)/shard_map/psum | solution.py:21
  106.5 10.8 %all-reduce.1 = (f32[]{:T(128)}, f32[768]{0:T(1024)S(1)}) all-reduce(f32[]{:T(128)} %get-tuple-element.10, f32[768]{0:T(1024)S(1)} %get-tuple-element.11), channel_id=1, replica_groups=mesh['section'=8,'shard_0'=16,'shard_1'=4,'shard_2'=2] {'shard_1'}, use_global_device_ids=true, to_apply=%region_7.0 | all-reduce | flops 769 | bytes 6152 | tf_op jit(solution)/shard_map/psum | solution.py:21
  117.3 3.1 %all-reduce.2 = (f32[]{:T(128)}, f32[768]{0:T(1024)S(1)}) all-reduce(f32[]{:T(128)} %get-tuple-element.12, f32[768]{0:T(1024)S(1)} %get-tuple-element.13), channel_id=1, replica_groups=mesh['section'=8,'shard_0'=16,'shard_1'=4,'shard_2'=2] {'shard_2'}, use_global_device_ids=true, to_apply=%region_8.9 | all-reduce | flops 769 | bytes 6152 | tf_op jit(solution)/shard_map/psum | solution.py:21
  120.4 1.0 bitcast_add_fusion
  121.5 4.4 %all-to-all-start = ((f32[8,96,128]{2,1,0:T(8,128)}), f32[8,96,128]{2,1,0:T(8,128)S(1)}, u32[]{:S(2)}, u32[]{:S(2)}) async-start(f32[8,96,128]{2,1,0:T(8,128)} %bitcast.22), calls=%async_computation | async-start | bytes 786432 | tf_op jit(solution)/shard_map/all_to_all | solution.py:93
  126.7 0.2 copy.15
  126.9 0.1 multiply_reduce_fusion
  127.0 0.6 copy-done.9
  127.6 13.4 %all-to-all-done = f32[8,96,128]{2,1,0:T(8,128)S(1)} async-done(((f32[8,96,128]{2,1,0:T(8,128)}), f32[8,96,128]{2,1,0:T(8,128)S(1)}, u32[]{:S(2)}, u32[]{:S(2)}) %all-to-all-start) | async-done | bytes 393248 | tf_op jit(solution)/shard_map/all_to_all | solution.py:93
  141.0 0.7 rev.10
  141.7 4.0 %all-to-all-start.1 = ((bf16[8,96,128]{2,1,0:T(8,128)(2,1)}), bf16[8,96,128]{2,1,0:T(8,128)(2,1)}, u32[]{:S(2)}, u32[]{:S(2)}) async-start(bf16[8,96,128]{2,1,0:T(8,128)(2,1)} %rev.10), calls=%async_computation.1 | async-start | bytes 393216 | tf_op jit(solution)/shard_map/all_to_all | solution.py:95
  145.7 0.7 broadcast_divide_fusion.1
  146.4 1.0 copy.23
  147.4 0.0 copy-done.4
  147.5 0.2 copy.21
  147.7 0.4 broadcast_divide_fusion
  148.1 1.0 copy.24
  149.1 1.0 copy.22
  150.1 6.6 %all-to-all-done.1 = bf16[8,96,128]{2,1,0:T(8,128)(2,1)} async-done(((bf16[8,96,128]{2,1,0:T(8,128)(2,1)}), bf16[8,96,128]{2,1,0:T(8,128)(2,1)}, u32[]{:S(2)}, u32[]{:S(2)}) %all-to-all-start.1) | async-done | bytes 196640 | tf_op jit(solution)/shard_map/all_to_all | solution.py:95
  156.6 1.6 %copy.38 = bf16[1,2,384,128]{3,2,1,0:T(8,128)(2,1)} copy(bf16[1,2,384,128]{3,2,1,0:T(8,128)(2,1)} %bitcast.23) | data formatting | bytes 393216
  (28 shorter events, 0.2 us)
Async XLA Ops:
  0.6 55.7 %copy-start = (bf16[1,2,384,512]{3,2,1,0:T(8,128)(2,1)S(1)}, bf16[1,2,384,512]{3,2,1,0:T(8,128)(2,1)}, u32[]{:S(2)}) copy-start(bf16[1,2,384,512]{3,2,1,0:T(8,128)(2,1)} %param.15) | copy-start | bytes 2359300
  0.6 55.7 %copy-start.1 = (bf16[1,2,384,128]{3,2,1,0:T(8,128)(2,1)S(1)}, bf16[1,2,384,128]{3,2,1,0:T(8,128)(2,1)}, u32[]{:S(2)}) copy-start(bf16[1,2,384,128]{3,2,1,0:T(8,128)(2,1)} %param.11) | copy-start | bytes 589828
  0.7 56.9 %copy-start.2 = (bf16[1,2,384,512]{3,2,1,0:T(8,128)(2,1)S(1)}, bf16[1,2,384,512]{3,2,1,0:T(8,128)(2,1)}, u32[]{:S(2)}) copy-start(bf16[1,2,384,512]{3,2,1,0:T(8,128)(2,1)} %param.14) | copy-start | bytes 2359300
  56.4 1.2 copy-start.10
  58.0 19.0 %copy-start.6 = (bf16[1,512,128]{2,1,0:T(8,128)(2,1)S(1)}, bf16[1,512,128]{2,1,0:T(8,128)(2,1)}, u32[]{:S(2)}) copy-start(bf16[1,512,128]{2,1,0:T(8,128)(2,1)} %param.16) | copy-start | bytes 393220
  77.0 0.9 copy-start.7
  77.9 42.5 %copy-start.5 = (bf16[2,384,128]{2,1,0:T(8,128)(2,1)S(1)}, bf16[2,384,128]{2,1,0:T(8,128)(2,1)}, u32[]{:S(2)}) copy-start(bf16[2,384,128]{2,1,0:T(8,128)(2,1)} %param.12) | copy-start | bytes 589828
  121.5 5.2 %copy-start.3 = (s32[1,2,512,128]{3,2,1,0:T(8,128)S(1)}, s32[1,2,512,128]{3,2,1,0:T(8,128)}, u32[]{:S(2)}) copy-start(s32[1,2,512,128]{3,2,1,0:T(8,128)} %param.18) | copy-start | bytes 1572868
  121.5 4.4 %copy-start.8 = (f32[1,2,512,1]{2,3,1,0:T(1,128)S(1)}, f32[1,2,512,1]{2,3,1,0:T(1,128)}, u32[]{:S(2)}) copy-start(f32[1,2,512,1]{2,3,1,0:T(1,128)} %param.20) | copy-start | bytes 12292
  121.5 19.5 %all-to-all-start = ((f32[8,96,128]{2,1,0:T(8,128)}), f32[8,96,128]{2,1,0:T(8,128)S(1)}, u32[]{:S(2)}, u32[]{:S(2)}) async-start(f32[8,96,128]{2,1,0:T(8,128)} %bitcast.22), calls=%async_computation | async-start | bytes 786432 | tf_op jit(solution)/shard_map/all_to_all | solution.py:93
  126.9 0.7 copy-start.9
  141.7 14.9 %all-to-all-start.1 = ((bf16[8,96,128]{2,1,0:T(8,128)(2,1)}), bf16[8,96,128]{2,1,0:T(8,128)(2,1)}, u32[]{:S(2)}, u32[]{:S(2)}) async-start(bf16[8,96,128]{2,1,0:T(8,128)(2,1)} %rev.10), calls=%async_computation.1 | async-start | bytes 393216 | tf_op jit(solution)/shard_map/all_to_all | solution.py:95
  146.4 1.0 copy-start.4
where the time goes:
time: 159 us; the launch traced here: 158 us
  blocking collectives  115 us (72%)
  waiting for transfers between devices  19.9 us (13%)
  starting transfers between devices  8.45 us (5%)
  local copies, waits for them, and re-layouts  6.95 us (4%)
  other arithmetic  4.27 us (3%)
  matrix products  2.4 us (2%)
    psum x7, blocking collectives, one_axis_at_a_time(): x = lax.psum(x, axis)  115 us
    all_to_all x1, waiting for transfers between devices, on_device(): lax.all_to_all(split_rows, 'section', split_axis=0, concat_axis=0, tiled=...  13.4 us
    all_to_all x1, waiting for transfers between devices, on_device(): lax.all_to_all(suffix, 'section', split_axis=0, concat_axis=0, tiled=True)  6.57 us
    unnamed x30, local copies, waits for them, and re-layouts  6.21 us
    all_to_all x1, starting transfers between devices, on_device(): lax.all_to_all(split_rows, 'section', split_axis=0, concat_axis=0, tiled=...  4.44 us
    all_to_all x1, starting transfers between devices, on_device(): lax.all_to_all(suffix, 'section', split_axis=0, concat_axis=0, tiled=True)  4.01 us
  transfers between devices with their start and end apart: 2, of which 2 were waited for; matrix products, arithmetic and copies ran while one was open for 3% of the time, Pallas kernels for 0%

commit v1 on v0

--- a/solution.py
+++ b/solution.py
@@ -4,11 +4,11 @@
 from jax.sharding import Mesh
 from jax.sharding import PartitionSpec as P
 
+
 D = 16384
 QB = 128
 STEP = 20
 SHARD = ("shard_0", "shard_1", "shard_2")
-SECTION_SHARD = ("section", "shard_0", "shard_1", "shard_2")
 
 
 beta_one = 0.9
@@ -16,10 +16,14 @@
 clip_norm = 1.0
 
 
-def one_axis_at_a_time(x, axes):
-    for axis in axes:
-        x = lax.psum(x, axis)
-    return x
+def gathered_sum(x, axes):
+    members = lax.axis_size(axes)
+    copies = jnp.broadcast_to(x[None], (members,) + x.shape)
+    return jnp.sum(exchange(copies, axes), axis=0)
+
+
+def exchange(x, axes):
+    return lax.all_to_all(x, axes, split_axis=0, concat_axis=0, tiled=True)
 
 
 def optimizer(gradients, square_total, first_codes, second_codes, first_scale, second_scale):
@@ -69,7 +73,6 @@
     width_local = top_grad.shape[2]
     row_count = micro_count * token_count
     section_count = lax.axis_size("section")
-    is_last = lax.axis_index("section") == section_count - 1
     inputs = section_inputs[0].reshape(row_count, width_local)
     inputs_f = inputs.astype(jnp.float32)
     gain = norm_gain[0]
@@ -78,25 +81,40 @@
     d_normed = jnp.dot(keys_rows, key_weight[0], preferred_element_type=jnp.float32) + jnp.dot(
         values_rows, value_weight[0], preferred_element_type=jnp.float32
     )
+    scaled_grad = gain * d_normed
     local_power = jnp.sum(inputs_f * inputs_f, axis=1)
-    local_dot = jnp.sum(inputs_f * gain * d_normed, axis=1)
-    power, row_dot = (one_axis_at_a_time(local_power, SHARD), one_axis_at_a_time(local_dot, SHARD))
+    local_dot = jnp.sum(inputs_f * scaled_grad, axis=1)
+    stats = jnp.stack([local_power, local_dot]).reshape(2 * row_count // 128, 128)
+    for axes in (("shard_1", "shard_2"), "shard_0"):
+        stats = gathered_sum(stats, axes)
+    power, row_dot = stats.reshape(2, row_count)
     root = 1.0 / jnp.sqrt(power / D + 1e-05)
     normed = (inputs_f * root[:, None] * gain).astype(jnp.bfloat16)
+    gradients = jnp.stack([project(keys_rows, normed), project(values_rows, normed)])
+    square_total = jnp.broadcast_to(jnp.sum(gradients * gradients), (1, 128))
+    for axes in ("section", SHARD):
+        square_total = gathered_sum(square_total, axes)
+    square_total = square_total[0, 0]
+    block_rows = row_count // section_count
     input_grad = (
-        gain * d_normed * root[:, None] - inputs_f * (root * root * root * row_dot / D)[:, None]
+        scaled_grad * root[:, None]
+        - inputs_f * (root * root * root * row_dot / D)[:, None]
     )
-    top_rows = top_grad.reshape(row_count, width_local).astype(jnp.float32)
-    base = input_grad + jnp.where(is_last, top_rows, jnp.zeros_like(top_rows))
-    block_rows = row_count // section_count
-    split_rows = base.reshape(section_count, block_rows, width_local)
-    by_section = lax.all_to_all(split_rows, "section", split_axis=0, concat_axis=0, tiled=True)
-    suffix = jnp.flip(jnp.cumsum(jnp.flip(by_section, 0), axis=0), 0).astype(jnp.bfloat16)
-    returned = lax.all_to_all(suffix, "section", split_axis=0, concat_axis=0, tiled=True)
-    leaving_rows = returned.reshape(row_count, width_local)
-    leaving = leaving_rows.reshape(1, micro_count, token_count, width_local)
-    gradients = jnp.stack([project(keys_rows, normed), project(values_rows, normed)])
-    square_total = one_axis_at_a_time(jnp.sum(gradients * gradients), SECTION_SHARD)
+    split_rows = input_grad.astype(jnp.bfloat16).reshape(
+        section_count, block_rows, width_local
+    )
+    by_section = exchange(split_rows, "section")
+    top_rows = lax.dynamic_slice_in_dim(
+        top_grad.reshape(row_count, width_local), lax.axis_index("section") * block_rows, block_rows
+    )
+    running = top_rows.astype(jnp.float32)
+    sums = [None] * section_count
+    for t in range(section_count - 1, -1, -1):
+        running = running + by_section[t].astype(jnp.float32)
+        sums[t] = running.astype(jnp.bfloat16)
+    suffix = jnp.stack(sums)
+    returned = exchange(suffix, "section")
+    leaving = returned.reshape(1, micro_count, token_count, width_local)
     direction, first_ratio, second_ratio = optimizer(
         gradients, square_total, first_codes[0], second_codes[0], first_scale[0], second_scale[0]
     )

time: 159 us -> 119 us (0.75)
  blocking collectives: 115 us -> 56.9 us
  other arithmetic: 4.27 us -> 9.95 us
  starting transfers between devices: 8.45 us -> 13.8 us
  waiting for transfers between devices: 19.9 us -> 23.9 us
  local copies, waits for them, and re-layouts: 6.95 us -> 10.2 us
    psum x7 -> x0, blocking collectives: 115 us -> none  [one_axis_at_a_time(): x = lax.psum(x, axis)]
    all_to_all x0 -> x3, blocking collectives: none -> 56.9 us  [exchange(): return lax.all_to_all(x, axes, split_axis=0, concat_axis=0, tiled=True)]
    all_to_all x2 -> x3, starting transfers between devices: 8.45 us -> 13.8 us  [exchange(): return lax.all_to_all(x, axes, split_axis=0, concat_axis=0, tiled=True)]
    unnamed x0 -> x7, other arithmetic: none -> 4.36 us
    all_to_all x2 -> x3, waiting for transfers between devices: 19.9 us -> 23.9 us  [exchange(): return lax.all_to_all(x, axes, split_axis=0, concat_axis=0, tiled=True)]
    unnamed x30 -> x33, local copies, waits for them, and re-layouts: 6.21 us -> 8.82 us
  transfers between devices with their start and end apart: 2 -> 3, of which waited for: 2 -> 3; matrix products, arithmetic and copies ran while one was open for 3% -> 7% of each run, Pallas kernels for 0% -> 0%
where the time goes in v1:
time: 119 us
  blocking collectives  56.9 us (48%)
  waiting for transfers between devices  23.9 us (20%)
  starting transfers between devices  13.8 us (12%)
  local copies, waits for them, and re-layouts  10.2 us (9%)
  other arithmetic  9.95 us (8%)
  matrix products  2.85 us (2%)
    all_to_all x3, blocking collectives, exchange(): return lax.all_to_all(x, axes, split_axis=0, concat_axis=0, tiled=True)  56.9 us
    all_to_all x3, waiting for transfers between devices, exchange(): return lax.all_to_all(x, axes, split_axis=0, concat_axis=0, tiled=True)  23.9 us
    all_to_all x3, starting transfers between devices, exchange(): return lax.all_to_all(x, axes, split_axis=0, concat_axis=0, tiled=True)  13.8 us
    unnamed x33, local copies, waits for them, and re-layouts  8.82 us
    unnamed x7, other arithmetic  4.36 us
  transfers between devices with their start and end apart: 3, of which 3 were waited for; matrix products, arithmetic and copies ran while one was open for 7% of the time, Pallas kernels for 0%

profile of v1, /device:TPU:2, one launch (start us, length us, event | category | flops | bytes accessed | tf_op | source)
XLA Modules:
  0.0 118.6 jit_solution(6073325206472001800)
XLA Ops:
  0.7 1.2 %fusion.22 = f32[2,384]{1,0:T(2,128)S(1)} fusion(bf16[1,2,384,128]{3,2,1,0:T(8,128)(2,1)} %param.11), kind=kLoop, calls=%fused_computation.40 | loop fusion | flops 294144 | bytes 199680 | tf_op jit(solution)/shard_map/reduce_sum | solution.py:85
  1.9 1.5 %fusion.32 = f32[768,128]{1,0:T(8,128)S(1)} fusion(bf16[768,512]{1,0:T(8,128)(2,1)} %bitcast.189, bf16[1,512,128]{2,1,0:T(8,128)(2,1)S(1)} %copy-done.6), kind=kOutput, calls=%fused_computation.50 | convolution fusion | flops 100663296 | bytes 1310720 | tf_op jit(solution)/shard_map/dot_general | solution.py:81
  3.5 0.6 copy-done.11
  4.6 19.7 %all_to_all.30 = f32[8,12,128]{2,1,0:T(8,128)S(1)} all-to-all(f32[8,12,128]{2,1,0:T(8,128)S(1)} %broadcast_in_dim.9), channel_id=1, replica_groups=mesh['section'=8,'shard_0'=16,'shard_1'=4,'shard_2'=2] {'shard_1','shard..., dimensions={0} | all-to-all | bytes 98304 | tf_op jit(solution)/shard_map/all_to_all | solution.py:26
  24.4 22.6 %all_to_all.31 = f32[16,12,128]{2,1,0:T(8,128)S(1)} all-to-all(f32[16,12,128]{2,1,0:T(8,128)S(1)} %broadcast_in_dim.10), channel_id=1, replica_groups=mesh['section'=8,'shard_0'=16,'shard_1'=4,'shard_2'=2] {'shard_0'}, dimensions={0} | all-to-all | bytes 196608 | tf_op jit(solution)/shard_map/all_to_all | solution.py:26
  47.9 0.7 fusion.17
  48.6 0.6 broadcast_in_dim_broadcast_in_dim_broadcast_in_dim.3
  49.3 14.6 %all_to_all.32 = f32[8,1,128]{2,1,0:T(1,128)S(1)} all-to-all(f32[8,1,128]{2,1,0:T(1,128)S(1)} %broadcast_in_dim_broadcast_in_dim_broadcast_in_dim.3), channel_id=1, replica_groups=mesh['section'=8,'shard_0'=16,'shard_1'=4,'shard_2'=2] {'section'}, dimensions={0} | all-to-all | bytes 8192 | tf_op jit(solution)/shard_map/all_to_all | solution.py:26
  63.9 0.7 broadcast_in_dim.11
  64.6 7.0 %all-to-all-start.3 = ((f32[128,1,128]{2,1,0:T(1,128)}), f32[128,1,128]{2,1,0:T(1,128)S(1)}, u32[]{:S(2)}, u32[]{:S(2)}) async-start(f32[128,1,128]{2,1,0:T(1,128)} %broadcast_in_dim.11), calls=%async_computation.3 | async-start | bytes 131072 | tf_op jit(solution)/shard_map/all_to_all | solution.py:26
  71.6 1.0 fusion.27
  72.6 12.9 %all-to-all-done.3 = f32[128,1,128]{2,1,0:T(1,128)S(1)} async-done(((f32[128,1,128]{2,1,0:T(1,128)}), f32[128,1,128]{2,1,0:T(1,128)S(1)}, u32[]{:S(2)}, u32[]{:S(2)}) %all-to-all-start.3) | async-done | bytes 65568 | tf_op jit(solution)/shard_map/all_to_all | solution.py:26
  85.5 3.4 %all-to-all-start.4 = ((bf16[8,96,128]{2,1,0:T(8,128)(2,1)}), bf16[8,96,128]{2,1,0:T(8,128)(2,1)S(1)}, u32[]{:S(2)}, u32[]{:S(2)}) async-start(bf16[8,96,128]{2,1,0:T(8,128)(2,1)} %bitcast.28), calls=%async_computation.4 | async-start | bytes 393216 | tf_op jit(solution)/shard_map/all_to_all | solution.py:26
  88.9 0.7 copy-done.10
  89.6 0.7 copy-done.9
  90.5 0.8 copy-done.5
  91.3 1.0 copy.45
  92.6 7.2 %all-to-all-done.4 = bf16[8,96,128]{2,1,0:T(8,128)(2,1)S(1)} async-done(((bf16[8,96,128]{2,1,0:T(8,128)(2,1)}), bf16[8,96,128]{2,1,0:T(8,128)(2,1)S(1)}, u32[]{:S(2)}, u32[]{:S(2)}) %all-to-all-start.4) | async-done | bytes 196640 | tf_op jit(solution)/shard_map/all_to_all | solution.py:26
  99.8 0.6 fusion.48
  100.5 0.6 fusion.40
  101.1 0.6 bitcast_dynamic-update-slice_fusion.2
  102.9 0.6 fusion.44
  103.6 0.6 bitcast_dynamic-update-slice_fusion
  104.2 0.6 fusion.46
  104.8 3.4 %all-to-all-start.5 = ((bf16[8,96,128]{2,1,0:T(8,128)(2,1)}), bf16[8,96,128]{2,1,0:T(8,128)(2,1)S(1)}, u32[]{:S(2)}, u32[]{:S(2)}) async-start(bf16[8,96,128]{2,1,0:T(8,128)(2,1)} %fusion.46), calls=%async_computation.5 | async-start | bytes 393216 | tf_op jit(solution)/shard_map/all_to_all | solution.py:26
  108.2 0.7 broadcast_divide_fusion.1
  108.9 1.0 copy.47
  109.9 1.2 %broadcast_divide_fusion = (f32[1,2,512,128]{2,3,1,0:T(8,128)}, f32[1,2,512,128]{2,3,1,0:T(8,128)S(1)}) fusion(f32[2,512]{1,0:T(2,128)S(1)} %get-tuple-element.28, f32[1,1,512,128]{2,3,1,0:T(8,128)S(1)} %bitcast.184, f32[1,1,512,128]{2,3,1,0:T(8,128)S(1)} %bitcast.188, f32[]{:T(128)} %bitcast.18, s32[1,2,512,128]{2,3,1,0:T(8,128)S(1)} %copy-done.3, ...), kind=kLoop, calls=%fused_computation.46 | loop fusion | flops 1966080 | bytes 2629636 | tf_op jit(solution)/shard_map/div | solution.py:48
  111.1 2.0 %copy.48 = f32[1,2,512,128]{3,2,1,0:T(8,128)} copy(f32[1,2,512,128]{2,3,1,0:T(8,128)} %get-tuple-element.22) | data formatting | bytes 1048576
  113.2 1.0 copy.46
  114.2 3.8 %all-to-all-done.5 = bf16[8,96,128]{2,1,0:T(8,128)(2,1)S(1)} async-done(((bf16[8,96,128]{2,1,0:T(8,128)(2,1)}), bf16[8,96,128]{2,1,0:T(8,128)(2,1)S(1)}, u32[]{:S(2)}, u32[]{:S(2)}) %all-to-all-start.5) | async-done | bytes 196640 | tf_op jit(solution)/shard_map/all_to_all | solution.py:26
  118.0 0.7 copy.74
  (43 shorter events, 3.1 us)
Async XLA Ops:
  0.6 2.8 %copy-start = (bf16[1,2,384,512]{3,2,1,0:T(8,128)(2,1)S(1)}, bf16[1,2,384,512]{3,2,1,0:T(8,128)(2,1)}, u32[]{:S(2)}) copy-start(bf16[1,2,384,512]{3,2,1,0:T(8,128)(2,1)} %param.15) | copy-start | bytes 2359300
  0.6 1.2 %copy-start.6 = (bf16[1,512,128]{2,1,0:T(8,128)(2,1)S(1)}, bf16[1,512,128]{2,1,0:T(8,128)(2,1)}, u32[]{:S(2)}) copy-start(bf16[1,512,128]{2,1,0:T(8,128)(2,1)} %param.16) | copy-start | bytes 393220
  1.9 1.6 %copy-start.1 = (bf16[1,2,384,128]{3,2,1,0:T(8,128)(2,1)S(1)}, bf16[1,2,384,128]{3,2,1,0:T(8,128)(2,1)}, u32[]{:S(2)}) copy-start(bf16[1,2,384,128]{3,2,1,0:T(8,128)(2,1)} %param.11) | copy-start | bytes 589828
  1.9 1.6 %copy-start.7 = (bf16[1,512,128]{2,1,0:T(8,128)(2,1)S(1)}, bf16[1,512,128]{2,1,0:T(8,128)(2,1)}, u32[]{:S(2)}) copy-start(bf16[1,512,128]{2,1,0:T(8,128)(2,1)} %param.17) | copy-start | bytes 393220
  3.5 0.7 copy-start.11
  24.3 23.1 %copy-start.2 = (bf16[1,2,384,512]{3,2,1,0:T(8,128)(2,1)S(1)}, bf16[1,2,384,512]{3,2,1,0:T(8,128)(2,1)}, u32[]{:S(2)}) copy-start(bf16[1,2,384,512]{3,2,1,0:T(8,128)(2,1)} %param.14) | copy-start | bytes 2359300
  64.6 20.9 %all-to-all-start.3 = ((f32[128,1,128]{2,1,0:T(1,128)}), f32[128,1,128]{2,1,0:T(1,128)S(1)}, u32[]{:S(2)}, u32[]{:S(2)}) async-start(f32[128,1,128]{2,1,0:T(1,128)} %broadcast_in_dim.11), calls=%async_computation.3 | async-start | bytes 131072 | tf_op jit(solution)/shard_map/all_to_all | solution.py:26
  71.6 18.7 %copy-start.4 = (s32[1,2,512,128]{3,2,1,0:T(8,128)S(1)}, s32[1,2,512,128]{3,2,1,0:T(8,128)}, u32[]{:S(2)}) copy-start(s32[1,2,512,128]{3,2,1,0:T(8,128)} %param.18) | copy-start | bytes 1572868
  85.5 14.3 %all-to-all-start.4 = ((bf16[8,96,128]{2,1,0:T(8,128)(2,1)}), bf16[8,96,128]{2,1,0:T(8,128)(2,1)S(1)}, u32[]{:S(2)}, u32[]{:S(2)}) async-start(bf16[8,96,128]{2,1,0:T(8,128)(2,1)} %bitcast.28), calls=%async_computation.4 | async-start | bytes 393216 | tf_op jit(solution)/shard_map/all_to_all | solution.py:26
  88.9 0.7 copy-start.10
  89.6 0.7 copy-start.9
  90.3 1.0 copy-start.5
  92.5 7.3 %copy-start.8 = (bf16[2,384,128]{2,1,0:T(8,128)(2,1)S(1)}, bf16[2,384,128]{2,1,0:T(8,128)(2,1)}, u32[]{:S(2)}) copy-start(bf16[2,384,128]{2,1,0:T(8,128)(2,1)} %param.12) | copy-start | bytes 589828
  104.8 13.2 %all-to-all-start.5 = ((bf16[8,96,128]{2,1,0:T(8,128)(2,1)}), bf16[8,96,128]{2,1,0:T(8,128)(2,1)S(1)}, u32[]{:S(2)}, u32[]{:S(2)}) async-start(bf16[8,96,128]{2,1,0:T(8,128)(2,1)} %fusion.46), calls=%async_computation.5 | async-start | bytes 393216 | tf_op jit(solution)/shard_map/all_to_all | solution.py:26
  108.9 1.0 copy-start.3

commit v2 on v0

v2 whole, which is shorter than its diff:
```python
import jax
import jax.numpy as jnp
from jax import lax
from jax.experimental import pallas as pl
from jax.experimental.pallas import tpu as pltpu
from jax.sharding import Mesh
from jax.sharding import PartitionSpec as P


D = 16384
STEP = 20
SHARD = ("shard_0", "shard_1", "shard_2")
SIDE = 128
TAIL = 16

beta_one = 0.9
beta_two = 0.95
clip_norm = 1.0

F32 = jnp.float32
BF16 = jnp.bfloat16


def kernel_call(body, out_shape, flops, moved, room=16 * 2**20, **options):
    return pl.pallas_call(
        body,
        out_shape=out_shape,
        compiler_params=pltpu.CompilerParams(vmem_limit_bytes=room),
        cost_estimate=pl.CostEstimate(flops=flops, bytes_accessed=moved, transcendentals=0),
        **options,
    )


def shape(dims, dtype=F32):
    return jax.ShapeDtypeStruct(dims, dtype)


def exchange(x, axes):
    return lax.all_to_all(x, axes, split_axis=0, concat_axis=0, tiled=True)


def turned_column(row):
    return jnp.transpose(jnp.broadcast_to(row, (SIDE, SIDE)))


def stats_body(x, gain, keys, values, key_w, value_w, copies, x_turned, u_turned):
    gain_column = turned_column(gain[...])
    blocks = x.shape[0] // SIDE
    for block in range(blocks):
        rows = pl.ds(block * SIDE, SIDE)
        grad = jnp.dot(keys[rows, :], key_w[...], preferred_element_type=F32)
        grad = grad + jnp.dot(values[rows, :], value_w[...], preferred_element_type=F32)
        x_block = jnp.transpose(x[rows, :].astype(F32))
        u_block = gain_column * jnp.transpose(grad)
        x_turned[:, rows] = x_block.astype(BF16)
        u_turned[:, rows] = u_block
        copies[0, pl.ds(block, 1), :] = jnp.sum(x_block * x_block, axis=0, keepdims=True)
        copies[0, pl.ds(blocks + block, 1), :] = jnp.sum(x_block * u_block, axis=0, keepdims=True)
    own = copies[0]
    for member in range(1, copies.shape[0]):
        copies[member] = own


def spread_body(parts, copies):
    total = parts[0]
    for member in range(1, parts.shape[0]):
        total = total + parts[member]
    copies[...] = jnp.broadcast_to(total[None], copies.shape)


def summed(parts):
    total = parts[0]
    for member in range(1, parts.shape[0]):
        total = total + parts[member]
    return total


def roots(power):
    return 1.0 / jnp.sqrt(power / D + 1e-05)


def gradient_body(
    parts, x_turned, u_turned, gain, keys, values, key_g, value_g, payload, normed
):
    stats = summed(parts)
    blocks = stats.shape[0] // 2
    root = roots(stats[:blocks])
    gain_column = turned_column(gain[...])
    for block in range(blocks):
        rows = pl.ds(block * SIDE, SIDE)
        scaled = x_turned[:, rows].astype(F32) * root[block : block + 1] * gain_column
        normed[:, rows] = scaled.astype(BF16)
    key_g[...] = jnp.dot(normed[...], keys[...], preferred_element_type=F32)
    value_g[...] = jnp.dot(normed[...], values[...], preferred_element_type=F32)
    squares = key_g[...] * key_g[...] + value_g[...] * value_g[...]
    row = jnp.sum(squares, axis=0, keepdims=True)
    lanes = row[:, :SIDE]
    for start in range(SIDE, row.shape[1], SIDE):
        lanes = lanes + row[:, start : start + SIDE]
    factor = root * root * root * stats[blocks:] / D
    sections, padded_rows, width = payload.shape
    block_rows = padded_rows - TAIL
    for block in range(blocks):
        rows = pl.ds(block * SIDE, SIDE)
        grad = (
            u_turned[:, rows] * root[block : block + 1]
            - x_turned[:, rows].astype(F32) * factor[block : block + 1]
        )
        grad = jnp.transpose(grad).astype(BF16)
        done = 0
        while done < SIDE:
            section, offset = divmod(block * SIDE + done, block_rows)
            count = min(SIDE - done, block_rows - offset)
            payload[section, pl.ds(offset, count), :] = grad[done : done + count]
            done += count
    tail = lax.broadcasted_iota(jnp.int32, (TAIL, width), 0)
    high = lanes.astype(BF16).astype(F32)
    middle = (lanes - high).astype(BF16).astype(F32)
    low = lanes - high - middle
    pieces = jnp.where(tail == 0, high, 0.0)
    pieces = jnp.where(tail == 1, middle, pieces)
    pieces = jnp.where(tail == 2, low, pieces).astype(BF16)
    for section in range(sections):
        payload[section, pl.ds(block_rows, TAIL), :] = pieces


def square_spread_body(received, copies):
    start = received.shape[1] - TAIL
    pieces = received[0, pl.ds(start, TAIL), :].astype(F32)
    for member in range(1, received.shape[0]):
        pieces = pieces + received[member, pl.ds(start, TAIL), :].astype(F32)
    lanes = jnp.sum(pieces, axis=0, keepdims=True)
    copies[...] = jnp.broadcast_to(lanes[None], copies.shape)


def suffix_body(by_section, top, out):
    running = top[...].astype(F32)
    for section in range(by_section.shape[0] - 1, -1, -1):
        running = running + by_section[section, pl.ds(0, top.shape[0]), :].astype(F32)
        out[section] = running.astype(BF16)


def first_body(key_g, value_g, codes, scale, grads, old, largest):
    for kind, turned in enumerate((key_g, value_g)):
        largest[kind] = jnp.max(jnp.abs(turned[...]), axis=0, keepdims=True)
        for start in range(0, turned.shape[1], SIDE):
            rows = pl.ds(start, SIDE)
            grads[kind, rows, :] = jnp.transpose(turned[:, rows])
            code = codes[kind, rows, :]
            sign_part = jnp.where(code >= 8, -beta_one, beta_one)
            scales = turned_column(scale[kind, :, rows])
            old[kind, rows, :] = scales * sign_part * jnp.exp2(-(code & 7).astype(F32))


def second_body(codes, scale, old):
    for kind in range(codes.shape[0]):
        for start in range(0, codes.shape[1], SIDE):
            rows = pl.ds(start, SIDE)
            scales = turned_column(beta_two * scale[kind, :, rows])
            old[kind, rows, :] = scales * jnp.exp2(-codes[kind, rows, :].astype(F32))


def adam_body(
    parts, grads, first_old, second_old, first_scale, second_scale, largest, way, first, second
):
    total = jnp.sum(summed(parts), axis=1, keepdims=True)
    clip_factor = jnp.minimum(1.0, clip_norm / (jnp.sqrt(total) + 1e-06))
    bias_one = 1.0 - beta_one**STEP
    bias_two = 1.0 - beta_two**STEP
    edge = clip_factor * largest[0]
    first_part = 1.0 / (beta_one * first_scale[0] + (1.0 - beta_one) * edge)
    second_part = 1.0 / (beta_two * second_scale[0] + (1.0 - beta_two) * edge * edge)
    for start in range(0, grads.shape[1], SIDE):
        rows = pl.ds(start, SIDE)
        clipped = clip_factor * grads[0, rows, :]
        first_new = first_old[0, rows, :] + (1.0 - beta_one) * clipped
        second_new = second_old[0, rows, :] + (1.0 - beta_two) * clipped * clipped
        root = jnp.sqrt(second_new * (1.0 / bias_two)) + 1e-08
        way[0, rows, :] = first_new * (1.0 / bias_one) / root
        first[0, rows, :] = first_new * turned_column(first_part[:, start : start + SIDE])
        second[0, rows, :] = second_new * turned_column(second_part[:, start : start + SIDE])


def on_device(
    section_inputs,
    top_grad,
    norm_gain,
    key_grad,
    value_grad,
    key_weight,
    value_weight,
    first_codes,
    second_codes,
    first_scale,
    second_scale,
):
    micro_count, token_count, width = top_grad.shape
    row_count = micro_count * token_count
    features = key_grad.shape[3]
    sections = lax.axis_size("section")
    block_rows = row_count // sections
    stat_rows = 2 * row_count // SIDE
    x = section_inputs[0].reshape(row_count, width)
    keys = key_grad[0].reshape(row_count, features)
    values = value_grad[0].reshape(row_count, features)
    matmul = 2 * row_count * features * width
    slab = 4 * row_count * width
    moments = (2, features, width)
    moment_bytes = 4 * 2 * features * width

    copies, x_turned, u_turned = kernel_call(
        stats_body,
        (
            shape((lax.axis_size(("shard_1", "shard_2")), stat_rows, SIDE)),
            shape((width, row_count), BF16),
            shape((width, row_count)),
        ),
        2 * matmul,
        4 * slab,
        room=60 * 10**6,
    )(x, norm_gain, keys, values, key_weight[0], value_weight[0])
    parts = exchange(copies, ("shard_1", "shard_2"))
    copies = kernel_call(
        spread_body, shape((lax.axis_size("shard_0"), stat_rows, SIDE)), 2**14, 2**17
    )(parts)
    parts = exchange(copies, "shard_0")

    key_g, value_g, payload = kernel_call(
        gradient_body,
        (
            shape((width, features)),
            shape((width, features)),
            shape((sections, block_rows + TAIL, width), BF16),
        ),
        2 * matmul,
        4 * slab,
        scratch_shapes=[pltpu.VMEM((width, row_count), BF16)],
    )(parts, x_turned, u_turned, norm_gain, keys, values)
    received = exchange(payload, "section")
    copies = kernel_call(
        square_spread_body, shape((lax.axis_size(SHARD), 1, SIDE)), 2**14, 2**17
    )(received)
    squares = exchange(copies, SHARD)

    scale_rows = (2, 1, features)
    first_scales = first_scale.reshape(scale_rows)
    second_scales = second_scale.reshape(scale_rows)
    grads, first_old, largest = kernel_call(
        first_body,
        (shape(moments), shape(moments), shape(scale_rows)),
        moment_bytes,
        4 * moment_bytes,
    )(key_g, value_g, first_codes[0], first_scales)
    second_old = kernel_call(
        second_body, shape(moments), moment_bytes, 2 * moment_bytes
    )(second_codes[0], second_scales)

    top_rows = lax.dynamic_slice_in_dim(
        top_grad.reshape(row_count, width), lax.axis_index("section") * block_rows, block_rows
    )
    suffix = kernel_call(
        suffix_body, shape((sections, block_rows, width), BF16), slab, slab
    )(received, top_rows)
    returned = exchange(suffix, "section")
    leaving = returned.reshape(1, micro_count, token_count, width)

    whole = pl.BlockSpec(squares.shape, lambda kind: (0, 0, 0))
    one = pl.BlockSpec((1,) + moments[1:], lambda kind: (kind, 0, 0))
    row = pl.BlockSpec((1,) + scale_rows[1:], lambda kind: (kind, 0, 0))
    outputs = kernel_call(
        adam_body,
        (shape(moments),) * 3,
        20 * moment_bytes,
        6 * moment_bytes,
        grid=(2,),
        in_specs=[whole] + [one] * 3 + [row] * 3,
        out_specs=[one] * 3,
    )(squares, grads, first_old, second_old, first_scales, second_scales, largest)
    direction, first_ratio, second_ratio = outputs
    return (direction[None], first_ratio[None], second_ratio[None], leaving)


def solution(mesh):
    finer = Mesh(
        mesh.devices.reshape(mesh.shape["section"], 16, 4, 2),
        ("section", "shard_0", "shard_1", "shard_2"),
    )
    in_specs = (
        P("section", None, None, SHARD),
        P(None, None, SHARD),
        P("section", SHARD),
        P("section", None, None, None),
        P("section", None, None, None),
        P("section", None, SHARD),
        P("section", None, SHARD),
        P("section", None, None, SHARD),
        P("section", None, None, SHARD),
        P("section", None, None, SHARD),
        P("section", None, None, SHARD),
    )
    out_specs = (
        P("section", None, None, SHARD),
        P("section", None, None, SHARD),
        P("section", None, None, SHARD),
        P("section", None, None, SHARD),
    )
    return jax.shard_map(
        on_device, mesh=finer, in_specs=in_specs, out_specs=out_specs, check_vma=False
    )
```

time: 159 us -> 103 us (0.65)
  the two profiles are of different devices: /device:TPU:2 before, /device:TPU:1 now
where the time goes in v2:
time: 103 us; the launch traced here: 102 us
  blocking collectives  56.8 us (55%)
  waiting for transfers between devices  20.3 us (20%)
  starting transfers between devices  14.9 us (14%)
  Pallas kernels  7.28 us (7%)
  local copies, waits for them, and re-layouts  2.18 us (2%)
    all_to_all x3, blocking collectives, exchange(): return lax.all_to_all(x, axes, split_axis=0, concat_axis=0, tiled=True)  56.8 us
    all_to_all x2, waiting for transfers between devices, exchange(): return lax.all_to_all(x, axes, split_axis=0, concat_axis=0, tiled=True)  20.3 us
    all_to_all x2, starting transfers between devices, exchange(): return lax.all_to_all(x, axes, split_axis=0, concat_axis=0, tiled=True)  14.9 us
    pallas_call x1, Pallas kernels, on_device(): kernel_call(stats_body, (shape((lax.axis_size(('shard_1', 'shard_2')), st...  3.03 us
    unnamed x21, local copies, waits for them, and re-layouts  2.17 us
  transfers between devices with their start and end apart: 2, of which 2 were waited for; matrix products, arithmetic and copies ran while one was open for 0% of the time, Pallas kernels for 3%

profile of v2, /device:TPU:1, one launch (start us, length us, event | category | flops | bytes accessed | tf_op | source)
XLA Modules:
  0.0 102.3 jit_solution(10411859705663389098)
XLA Ops:
  0.6 0.0 copy-start
  0.6 0.0 copy-start.1
  0.7 0.0 copy-start.2
  0.7 3.0 %shard_map.138 = (f32[8,12,128]{2,1,0:T(8,128)}, bf16[128,768]{1,0:T(8,128)(2,1)}, f32[128,768]{1,0:T(8,128)}) custom-call(bf16[768,128]{1,0:T(8,128)(2,1)} %bitcast.26, f32[1,128]{1,0:T(1,128)} %gain.3, bf16[768,512]{1,0:T(8,128)(2,1)} %bitcast.15, bf16[768,512]{1,0:T(8,128)(2,1)} %bitcast.17, bf16[512,128]{1,0:T(8,128)(2,1)} %bitcast.27, ...), custom_call_target="tpu_custom_call" | custom-call | flops 201326592 | bytes 1572864 | tf_op jit(solution)/shard_map/pallas_call | solution.py:211
  3.7 0.0 copy-start.5
  3.7 22.3 %all_to_all.25.parts = f32[8,12,128]{2,1,0:T(8,128)S(1)} all-to-all(f32[8,12,128]{2,1,0:T(8,128)} %get-tuple-element.16), channel_id=1, replica_groups=mesh['section'=8,'shard_0'=16,'shard_1'=4,'shard_2'=2] {'shard_1','shard..., dimensions={0} | all-to-all | bytes 98304 | tf_op jit(solution)/shard_map/all_to_all | solution.py:39
  26.0 0.0 copy-start.6
  26.1 18.9 %all_to_all.26.parts = f32[16,12,128]{2,1,0:T(8,128)S(1)} all-to-all(f32[16,12,128]{2,1,0:T(8,128)S(1)} %shard_map.139), channel_id=1, replica_groups=mesh['section'=8,'shard_0'=16,'shard_1'=4,'shard_2'=2] {'shard_0'}, dimensions={0} | all-to-all | bytes 196608 | tf_op jit(solution)/shard_map/all_to_all | solution.py:39
  45.0 0.0 copy-done.1
  45.0 0.0 copy-done.2
  45.0 0.0 copy-done.5
  45.0 0.0 copy-done.6
  45.0 0.6 copy-done.9
  45.6 0.5 shard_map.140
  46.1 15.6 %all_to_all.27.received.by_section = bf16[8,112,128]{2,1,0:T(8,128)(2,1)S(1)} all-to-all(bf16[8,112,128]{2,1,0:T(8,128)(2,1)S(1)} %get-tuple-element.19), channel_id=1, replica_groups=mesh['section'=8,'shard_0'=16,'shard_1'=4,'shard_2'=2] {'section'}, dimensions={0} | all-to-all | bytes 458752 | tf_op jit(solution)/shard_map/all_to_all | solution.py:39
  61.7 0.7 shard_map.141
  62.4 11.4 %all-to-all-start.3 = ((f32[128,1,128]{2,1,0:T(1,128)}), f32[128,1,128]{2,1,0:T(1,128)S(1)}, u32[]{:S(2)}, u32[]{:S(2)}) async-start(f32[128,1,128]{2,1,0:T(1,128)} %shard_map.141), calls=%async_computation.3 | async-start | bytes 131072 | tf_op jit(solution)/shard_map/all_to_all | solution.py:39
  73.8 0.0 copy-done
  73.8 0.7 shard_map.145
  74.5 14.1 %all-to-all-done.3.parts = f32[128,1,128]{2,1,0:T(1,128)S(1)} async-done(((f32[128,1,128]{2,1,0:T(1,128)}), f32[128,1,128]{2,1,0:T(1,128)S(1)}, u32[]{:S(2)}, u32[]{:S(2)}) %all-to-all-start.3) | async-done | bytes 65568 | tf_op jit(solution)/shard_map/all_to_all | solution.py:39
  88.6 3.5 %all-to-all-start.4 = ((bf16[8,96,128]{2,1,0:T(8,128)(2,1)}), bf16[8,96,128]{2,1,0:T(8,128)(2,1)S(1)}, u32[]{:S(2)}, u32[]{:S(2)}) async-start(bf16[8,96,128]{2,1,0:T(8,128)(2,1)} %shard_map.145), calls=%async_computation.4 | async-start | bytes 393216 | tf_op jit(solution)/shard_map/all_to_all | solution.py:39
  92.1 0.0 copy-done.3
  92.1 0.0 copy-done.8
  92.2 0.0 copy-start.4
  92.2 0.2 shard_map.143.second_old
  92.4 0.0 copy-start.7
  92.4 0.8 copy-done.4
  93.2 0.0 copy-done.7
  93.2 0.3 shard_map.142
  93.6 1.8 %shard_map.144 = (f32[2,512,128]{2,1,0:T(8,128)}, f32[2,512,128]{2,1,0:T(8,128)}, f32[2,512,128]{2,1,0:T(8,128)}) custom-call(f32[128,1,128]{2,1,0:T(1,128)S(1)} %all-to-all-done.3.parts, f32[2,512,128]{2,1,0:T(8,128)S(1)} %get-tuple-element.22.grads, f32[2,512,128]{2,1,0:T(8,128)S(1)} %get-tuple-element.23.first_old, ...), custom_call_target="tpu_custom_call" | custom-call | flops 10485760 | bytes 3145728 | tf_op jit(solution)/shard_map/pallas_call | solution.py:270
  95.4 6.2 %all-to-all-done.4 = bf16[8,96,128]{2,1,0:T(8,128)(2,1)S(1)} async-done(((bf16[8,96,128]{2,1,0:T(8,128)(2,1)}), bf16[8,96,128]{2,1,0:T(8,128)(2,1)S(1)}, u32[]{:S(2)}, u32[]{:S(2)}) %all-to-all-start.4) | async-done | bytes 196640 | tf_op jit(solution)/shard_map/all_to_all | solution.py:39
  101.6 0.7 copy.16
  (5 shorter events, 0.0 us)
Async XLA Ops:
  0.6 73.1 %copy-start = (bf16[2,384,128]{2,1,0:T(8,128)(2,1)S(1)}, bf16[2,384,128]{2,1,0:T(8,128)(2,1)}, u32[]{:S(2)}) copy-start(bf16[2,384,128]{2,1,0:T(8,128)(2,1)} %param.12) | copy-start | bytes 589828
  0.6 44.3 %copy-start.1 = (bf16[1,2,384,512]{3,2,1,0:T(8,128)(2,1)S(1)}, bf16[1,2,384,512]{3,2,1,0:T(8,128)(2,1)}, u32[]{:S(2)}) copy-start(bf16[1,2,384,512]{3,2,1,0:T(8,128)(2,1)} %param.14) | copy-start | bytes 2359300
  0.7 44.3 %copy-start.2 = (bf16[1,2,384,512]{3,2,1,0:T(8,128)(2,1)S(1)}, bf16[1,2,384,512]{3,2,1,0:T(8,128)(2,1)}, u32[]{:S(2)}) copy-start(bf16[1,2,384,512]{3,2,1,0:T(8,128)(2,1)} %param.15) | copy-start | bytes 2359300
  3.7 41.3 %copy-start.5 = (f32[128,768]{1,0:T(8,128)S(1)}, f32[128,768]{1,0:T(8,128)}, u32[]{:S(2)}) copy-start(f32[128,768]{1,0:T(8,128)} %get-tuple-element.18.u_turned) | copy-start | bytes 1179652
  26.0 18.9 %copy-start.6 = (bf16[128,768]{1,0:T(8,128)(2,1)S(1)}, bf16[128,768]{1,0:T(8,128)(2,1)}, u32[]{:S(2)}) copy-start(bf16[128,768]{1,0:T(8,128)(2,1)} %get-tuple-element.17.x_turned) | copy-start | bytes 589828
  45.0 0.7 copy-start.9
  62.4 29.8 %copy-start.3 = (s32[1,2,512,128]{3,2,1,0:T(8,128)S(1)}, s32[1,2,512,128]{3,2,1,0:T(8,128)}, u32[]{:S(2)}) copy-start(s32[1,2,512,128]{3,2,1,0:T(8,128)} %param.19) | copy-start | bytes 1572868
  62.4 26.2 %all-to-all-start.3 = ((f32[128,1,128]{2,1,0:T(1,128)}), f32[128,1,128]{2,1,0:T(1,128)S(1)}, u32[]{:S(2)}, u32[]{:S(2)}) async-start(f32[128,1,128]{2,1,0:T(1,128)} %shard_map.141), calls=%async_computation.3 | async-start | bytes 131072 | tf_op jit(solution)/shard_map/all_to_all | solution.py:39
  88.6 3.5 %copy-start.8 = (f32[1,2,512,1]{2,3,1,0:T(1,128)S(1)}, f32[1,2,512,1]{2,3,1,0:T(1,128)}, u32[]{:S(2)}) copy-start(f32[1,2,512,1]{2,3,1,0:T(1,128)} %param.21) | copy-start | bytes 12292
  88.6 13.0 %all-to-all-start.4 = ((bf16[8,96,128]{2,1,0:T(8,128)(2,1)}), bf16[8,96,128]{2,1,0:T(8,128)(2,1)S(1)}, u32[]{:S(2)}, u32[]{:S(2)}) async-start(bf16[8,96,128]{2,1,0:T(8,128)(2,1)} %shard_map.145), calls=%async_computation.4 | async-start | bytes 393216 | tf_op jit(solution)/shard_map/all_to_all | solution.py:39
  92.2 1.0 %copy-start.4 = (s32[1,2,512,128]{3,2,1,0:T(8,128)S(1)}, s32[1,2,512,128]{3,2,1,0:T(8,128)}, u32[]{:S(2)}) copy-start(s32[1,2,512,128]{3,2,1,0:T(8,128)} %param.18) | copy-start | bytes 1572868
  92.4 0.8 copy-start.7

commit v3 on v2

--- a/solution.py
+++ b/solution.py
@@ -11,7 +11,7 @@
 STEP = 20
 SHARD = ("shard_0", "shard_1", "shard_2")
 SIDE = 128
-TAIL = 16
+TAIL = 8
 
 beta_one = 0.9
 beta_two = 0.95
@@ -80,7 +80,7 @@
 
 
 def gradient_body(
-    parts, x_turned, u_turned, gain, keys, values, key_g, value_g, payload, normed
+    parts, x_turned, u_turned, gain, keys, values, key_g, value_g, lanes, input_grad, normed
 ):
     stats = summed(parts)
     blocks = stats.shape[0] // 2
@@ -94,50 +94,50 @@
     value_g[...] = jnp.dot(normed[...], values[...], preferred_element_type=F32)
     squares = key_g[...] * key_g[...] + value_g[...] * value_g[...]
     row = jnp.sum(squares, axis=0, keepdims=True)
-    lanes = row[:, :SIDE]
+    total = row[:, :SIDE]
     for start in range(SIDE, row.shape[1], SIDE):
-        lanes = lanes + row[:, start : start + SIDE]
+        total = total + row[:, start : start + SIDE]
+    lanes[...] = total
     factor = root * root * root * stats[blocks:] / D
-    sections, padded_rows, width = payload.shape
-    block_rows = padded_rows - TAIL
     for block in range(blocks):
         rows = pl.ds(block * SIDE, SIDE)
         grad = (
             u_turned[:, rows] * root[block : block + 1]
             - x_turned[:, rows].astype(F32) * factor[block : block + 1]
         )
-        grad = jnp.transpose(grad).astype(BF16)
-        done = 0
-        while done < SIDE:
-            section, offset = divmod(block * SIDE + done, block_rows)
-            count = min(SIDE - done, block_rows - offset)
-            payload[section, pl.ds(offset, count), :] = grad[done : done + count]
-            done += count
+        input_grad[rows, :] = jnp.transpose(grad).astype(BF16)
+
+
+def suffix_body(by_section, top, lanes, payload):
+    sections, block_rows, width = by_section.shape
     tail = lax.broadcasted_iota(jnp.int32, (TAIL, width), 0)
-    high = lanes.astype(BF16).astype(F32)
-    middle = (lanes - high).astype(BF16).astype(F32)
-    low = lanes - high - middle
+    whole = lanes[...]
+    high = whole.astype(BF16).astype(F32)
+    middle = (whole - high).astype(BF16).astype(F32)
+    low = whole - high - middle
     pieces = jnp.where(tail == 0, high, 0.0)
     pieces = jnp.where(tail == 1, middle, pieces)
     pieces = jnp.where(tail == 2, low, pieces).astype(BF16)
-    for section in range(sections):
+    running = top[...].astype(F32)
+    for section in range(sections - 1, -1, -1):
+        running = running + by_section[section].astype(F32)
+        payload[section, pl.ds(0, block_rows), :] = running.astype(BF16)
         payload[section, pl.ds(block_rows, TAIL), :] = pieces
 
 
-def square_spread_body(received, copies):
-    start = received.shape[1] - TAIL
-    pieces = received[0, pl.ds(start, TAIL), :].astype(F32)
-    for member in range(1, received.shape[0]):
-        pieces = pieces + received[member, pl.ds(start, TAIL), :].astype(F32)
+def square_spread_body(returned, copies):
+    start = returned.shape[1] - TAIL
+    pieces = returned[0, pl.ds(start, TAIL), :].astype(F32)
+    for member in range(1, returned.shape[0]):
+        pieces = pieces + returned[member, pl.ds(start, TAIL), :].astype(F32)
     lanes = jnp.sum(pieces, axis=0, keepdims=True)
     copies[...] = jnp.broadcast_to(lanes[None], copies.shape)
 
 
-def suffix_body(by_section, top, out):
-    running = top[...].astype(F32)
-    for section in range(by_section.shape[0] - 1, -1, -1):
-        running = running + by_section[section, pl.ds(0, top.shape[0]), :].astype(F32)
-        out[section] = running.astype(BF16)
+def leaving_body(returned, out):
+    block_rows = out.shape[1]
+    for owner in range(out.shape[0]):
+        out[owner] = returned[owner, pl.ds(0, block_rows), :]
 
 
 def first_body(key_g, value_g, codes, scale, grads, old, largest):
@@ -225,22 +225,36 @@
     )(parts)
     parts = exchange(copies, "shard_0")
 
-    key_g, value_g, payload = kernel_call(
+    key_g, value_g, lanes, input_grad = kernel_call(
         gradient_body,
         (
             shape((width, features)),
             shape((width, features)),
-            shape((sections, block_rows + TAIL, width), BF16),
+            shape((1, SIDE)),
+            shape((row_count, width), BF16),
         ),
         2 * matmul,
         4 * slab,
         scratch_shapes=[pltpu.VMEM((width, row_count), BF16)],
     )(parts, x_turned, u_turned, norm_gain, keys, values)
-    received = exchange(payload, "section")
+    by_section = exchange(input_grad.reshape(sections, block_rows, width), "section")
+    lanes = lax.psum(lanes, "shard_2")
+    lanes = lax.psum(lanes, "shard_1")
+
+    top_rows = lax.dynamic_slice_in_dim(
+        top_grad.reshape(row_count, width), lax.axis_index("section") * block_rows, block_rows
+    )
+    payload = kernel_call(
+        suffix_body, shape((sections, block_rows + TAIL, width), BF16), slab, slab
+    )(by_section, top_rows, lanes)
+    returned = exchange(payload, "section")
     copies = kernel_call(
-        square_spread_body, shape((lax.axis_size(SHARD), 1, SIDE)), 2**14, 2**17
-    )(received)
-    squares = exchange(copies, SHARD)
+        square_spread_body, shape((lax.axis_size("shard_0"), 1, SIDE)), 2**14, 2**17
+    )(returned)
+    squares = exchange(copies, "shard_0")
+    leaving = kernel_call(
+        leaving_body, shape((sections, block_rows, width), BF16), slab, slab
+    )(returned).reshape(1, micro_count, token_count, width)
 
     scale_rows = (2, 1, features)
     first_scales = first_scale.reshape(scale_rows)
@@ -254,15 +268,6 @@
     second_old = kernel_call(
         second_body, shape(moments), moment_bytes, 2 * moment_bytes
     )(second_codes[0], second_scales)
-
-    top_rows = lax.dynamic_slice_in_dim(
-        top_grad.reshape(row_count, width), lax.axis_index("section") * block_rows, block_rows
-    )
-    suffix = kernel_call(
-        suffix_body, shape((sections, block_rows, width), BF16), slab, slab
-    )(received, top_rows)
-    returned = exchange(suffix, "section")
-    leaving = returned.reshape(1, micro_count, token_count, width)
 
     whole = pl.BlockSpec(squares.shape, lambda kind: (0, 0, 0))
     one = pl.BlockSpec((1,) + moments[1:], lambda kind: (kind, 0, 0))

time: 103 us -> 103 us (level)
  the two profiles are of different devices: /device:TPU:1 before, /device:TPU:2 now
where the time goes in v3:
time: 103 us; the launch traced here: 102 us
  blocking collectives  71.3 us (69%)
  starting transfers between devices  10.9 us (11%)
  waiting for transfers between devices  10.3 us (10%)
  Pallas kernels  7.57 us (7%)
  local copies, waits for them, and re-layouts  1.5 us (1%)
    all_to_all x3, blocking collectives, exchange(): return lax.all_to_all(x, axes, split_axis=0, concat_axis=0, tiled=True)  59.7 us
    all_to_all x2, starting transfers between devices, exchange(): return lax.all_to_all(x, axes, split_axis=0, concat_axis=0, tiled=True)  10.9 us
    all_to_all x2, waiting for transfers between devices, exchange(): return lax.all_to_all(x, axes, split_axis=0, concat_axis=0, tiled=True)  10.3 us
    psum x1, blocking collectives, on_device(): lanes = lax.psum(lanes, 'shard_1')  9.15 us
    pallas_call x1, Pallas kernels, on_device(): kernel_call(stats_body, (shape((lax.axis_size(('shard_1', 'shard_2')), st...  3.02 us
    psum x1, blocking collectives, on_device(): lanes = lax.psum(lanes, 'shard_2')  2.47 us
  transfers between devices with their start and end apart: 2, of which 1 were waited for; matrix products, arithmetic and copies ran while one was open for 0% of the time, Pallas kernels for 1%

profile of v3, /device:TPU:2, one launch (start us, length us, event | category | flops | bytes accessed | tf_op | source)
XLA Modules:
  0.0 102.4 jit_solution(2787917295638592818)
XLA Ops:
  0.6 0.0 copy-start
  0.6 0.0 copy-start.1
  0.7 0.0 copy-start.2
  0.7 3.0 %shard_map.138 = (f32[8,12,128]{2,1,0:T(8,128)}, bf16[128,768]{1,0:T(8,128)(2,1)}, f32[128,768]{1,0:T(8,128)}) custom-call(bf16[768,128]{1,0:T(8,128)(2,1)} %bitcast.26, f32[1,128]{1,0:T(1,128)} %gain.3, bf16[768,512]{1,0:T(8,128)(2,1)} %bitcast.16, bf16[768,512]{1,0:T(8,128)(2,1)} %bitcast.18, bf16[512,128]{1,0:T(8,128)(2,1)} %bitcast.28, ...), custom_call_target="tpu_custom_call" | custom-call | flops 201326592 | bytes 1572864 | tf_op jit(solution)/shard_map/pallas_call | solution.py:211
  3.7 0.0 copy-start.5
  3.7 20.7 %all_to_all.25.parts = f32[8,12,128]{2,1,0:T(8,128)S(1)} all-to-all(f32[8,12,128]{2,1,0:T(8,128)} %get-tuple-element.17), channel_id=1, replica_groups=mesh['section'=8,'shard_0'=16,'shard_1'=4,'shard_2'=2] {'shard_1','shard..., dimensions={0} | all-to-all | bytes 98304 | tf_op jit(solution)/shard_map/all_to_all | solution.py:39
  24.4 21.9 %all_to_all.26.parts = f32[16,12,128]{2,1,0:T(8,128)S(1)} all-to-all(f32[16,12,128]{2,1,0:T(8,128)S(1)} %shard_map.139), channel_id=1, replica_groups=mesh['section'=8,'shard_0'=16,'shard_1'=4,'shard_2'=2] {'shard_0'}, dimensions={0} | all-to-all | bytes 196608 | tf_op jit(solution)/shard_map/all_to_all | solution.py:39
  46.3 0.0 copy-done.1
  46.4 0.0 copy-done.2
  46.4 0.0 copy-done.5
  46.4 0.0 copy-done.6
  46.4 0.6 copy-done.9
  47.0 1.1 %shard_map.140 = (f32[128,512]{1,0:T(8,128)S(1)}, f32[128,512]{1,0:T(8,128)S(1)}, f32[1,128]{1,0:T(1,128)S(1)}, bf16[768,128]{1,0:T(8,128)(2,1)}) custom-call(f32[16,12,128]{2,1,0:T(8,128)S(1)} %all_to_all.26.parts, bf16[128,768]{1,0:T(8,128)(2,1)S(1)} %copy-done.6, f32[128,768]{1,0:T(8,128)S(1)} %copy-done.5, f32[1,128]{1,0:T(1,128)S(1)} %copy-done.9, ...), custom_call_target="tpu_custom_call" | custom-call | flops 201326592 | bytes 1572864 | tf_op jit(solution)/shard_map/pallas_call | solution.py:228
  48.1 7.1 %all-to-all-start.2 = ((bf16[8,96,128]{2,1,0:T(8,128)(2,1)}), bf16[8,96,128]{2,1,0:T(8,128)(2,1)S(1)}, u32[]{:S(2)}, u32[]{:S(2)}) async-start(bf16[8,96,128]{2,1,0:T(8,128)(2,1)} %bitcast.5), calls=%async_computation.2 | async-start | bytes 393216 | tf_op jit(solution)/shard_map/all_to_all | solution.py:39
  55.2 0.0 copy-done
  55.2 2.5 %psum.14 = f32[1,128]{1,0:T(1,128)S(1)} all-reduce(f32[1,128]{1,0:T(1,128)S(1)} %get-tuple-element.21), channel_id=1, replica_groups=mesh['section'=8,'shard_0'=16,'shard_1'=4,'shard_2'=2] {'shard_2'}, use_global_device_ids=true, to_apply=%region_0.0 | all-reduce | flops 128 | bytes 1024 | tf_op jit(solution)/shard_map/psum | solution.py:241
  57.7 9.2 %psum.15.lanes = f32[1,128]{1,0:T(1,128)S(1)} all-reduce(f32[1,128]{1,0:T(1,128)S(1)} %psum.14), channel_id=1, replica_groups=mesh['section'=8,'shard_0'=16,'shard_1'=4,'shard_2'=2] {'shard_1'}, use_global_device_ids=true, to_apply=%region_1.0 | all-reduce | flops 128 | bytes 1024 | tf_op jit(solution)/shard_map/psum | solution.py:242
  66.8 0.0 all-to-all-done.2.by_section
  66.9 17.1 %all_to_all.27.returned = bf16[8,104,128]{2,1,0:T(8,128)(2,1)S(1)} all-to-all(bf16[8,104,128]{2,1,0:T(8,128)(2,1)S(1)} %shard_map.141), channel_id=1, replica_groups=mesh['section'=8,'shard_0'=16,'shard_1'=4,'shard_2'=2] {'section'}, dimensions={0} | all-to-all | bytes 425984 | tf_op jit(solution)/shard_map/all_to_all | solution.py:39
  84.0 0.6 shard_map.142
  84.6 3.8 %all-to-all-start.4 = ((f32[16,1,128]{2,1,0:T(1,128)}), f32[16,1,128]{2,1,0:T(1,128)S(1)}, u32[]{:S(2)}, u32[]{:S(2)}) async-start(f32[16,1,128]{2,1,0:T(1,128)} %shard_map.142), calls=%async_computation.4 | async-start | bytes 16384 | tf_op jit(solution)/shard_map/all_to_all | solution.py:39
  88.4 0.0 copy-done.3
  88.5 0.0 copy-done.8
  88.5 0.0 copy-start.4
  88.5 0.2 shard_map.144.second_old
  88.7 0.0 copy-start.7
  88.7 0.8 copy-done.4
  89.5 0.0 copy-done.7
  89.5 0.3 shard_map.143
  89.9 0.7 shard_map.146
  90.6 10.3 %all-to-all-done.4.parts = f32[16,1,128]{2,1,0:T(1,128)S(1)} async-done(((f32[16,1,128]{2,1,0:T(1,128)}), f32[16,1,128]{2,1,0:T(1,128)S(1)}, u32[]{:S(2)}, u32[]{:S(2)}) %all-to-all-start.4) | async-done | bytes 8224 | tf_op jit(solution)/shard_map/all_to_all | solution.py:39
  100.8 1.6 %shard_map.145 = (f32[2,512,128]{2,1,0:T(8,128)}, f32[2,512,128]{2,1,0:T(8,128)}, f32[2,512,128]{2,1,0:T(8,128)}) custom-call(f32[16,1,128]{2,1,0:T(1,128)S(1)} %all-to-all-done.4.parts, f32[2,512,128]{2,1,0:T(8,128)S(1)} %get-tuple-element.24.grads, f32[2,512,128]{2,1,0:T(8,128)S(1)} %get-tuple-element.25.first_old, ...), custom_call_target="tpu_custom_call" | custom-call | flops 10485760 | bytes 3145728 | tf_op jit(solution)/shard_map/pallas_call | solution.py:275
  (7 shorter events, 0.1 us)
Async XLA Ops:
  0.6 54.6 %copy-start = (bf16[2,384,128]{2,1,0:T(8,128)(2,1)S(1)}, bf16[2,384,128]{2,1,0:T(8,128)(2,1)}, u32[]{:S(2)}) copy-start(bf16[2,384,128]{2,1,0:T(8,128)(2,1)} %param.12) | copy-start | bytes 589828
  0.6 45.7 %copy-start.1 = (bf16[1,2,384,512]{3,2,1,0:T(8,128)(2,1)S(1)}, bf16[1,2,384,512]{3,2,1,0:T(8,128)(2,1)}, u32[]{:S(2)}) copy-start(bf16[1,2,384,512]{3,2,1,0:T(8,128)(2,1)} %param.14) | copy-start | bytes 2359300
  0.7 45.7 %copy-start.2 = (bf16[1,2,384,512]{3,2,1,0:T(8,128)(2,1)S(1)}, bf16[1,2,384,512]{3,2,1,0:T(8,128)(2,1)}, u32[]{:S(2)}) copy-start(bf16[1,2,384,512]{3,2,1,0:T(8,128)(2,1)} %param.15) | copy-start | bytes 2359300
  3.7 42.7 %copy-start.5 = (f32[128,768]{1,0:T(8,128)S(1)}, f32[128,768]{1,0:T(8,128)}, u32[]{:S(2)}) copy-start(f32[128,768]{1,0:T(8,128)} %get-tuple-element.19.u_turned) | copy-start | bytes 1179652
  24.4 22.0 %copy-start.6 = (bf16[128,768]{1,0:T(8,128)(2,1)S(1)}, bf16[128,768]{1,0:T(8,128)(2,1)}, u32[]{:S(2)}) copy-start(bf16[128,768]{1,0:T(8,128)(2,1)} %get-tuple-element.18.x_turned) | copy-start | bytes 589828
  46.3 0.7 copy-start.9
  48.1 18.8 %all-to-all-start.2 = ((bf16[8,96,128]{2,1,0:T(8,128)(2,1)}), bf16[8,96,128]{2,1,0:T(8,128)(2,1)S(1)}, u32[]{:S(2)}, u32[]{:S(2)}) async-start(bf16[8,96,128]{2,1,0:T(8,128)(2,1)} %bitcast.5), calls=%async_computation.2 | async-start | bytes 393216 | tf_op jit(solution)/shard_map/all_to_all | solution.py:39
  66.8 21.6 %copy-start.3 = (s32[1,2,512,128]{3,2,1,0:T(8,128)S(1)}, s32[1,2,512,128]{3,2,1,0:T(8,128)}, u32[]{:S(2)}) copy-start(s32[1,2,512,128]{3,2,1,0:T(8,128)} %param.19) | copy-start | bytes 1572868
  84.6 3.9 %copy-start.8 = (f32[1,2,512,1]{2,3,1,0:T(1,128)S(1)}, f32[1,2,512,1]{2,3,1,0:T(1,128)}, u32[]{:S(2)}) copy-start(f32[1,2,512,1]{2,3,1,0:T(1,128)} %param.21) | copy-start | bytes 12292
  84.6 16.3 %all-to-all-start.4 = ((f32[16,1,128]{2,1,0:T(1,128)}), f32[16,1,128]{2,1,0:T(1,128)S(1)}, u32[]{:S(2)}, u32[]{:S(2)}) async-start(f32[16,1,128]{2,1,0:T(1,128)} %shard_map.142), calls=%async_computation.4 | async-start | bytes 16384 | tf_op jit(solution)/shard_map/all_to_all | solution.py:39
  88.5 1.0 %copy-start.4 = (s32[1,2,512,128]{3,2,1,0:T(8,128)S(1)}, s32[1,2,512,128]{3,2,1,0:T(8,128)}, u32[]{:S(2)}) copy-start(s32[1,2,512,128]{3,2,1,0:T(8,128)} %param.18) | copy-start | bytes 1572868
  88.7 0.8 copy-start.7

commit v4 on v3

--- a/solution.py
+++ b/solution.py
@@ -11,7 +11,6 @@
 STEP = 20
 SHARD = ("shard_0", "shard_1", "shard_2")
 SIDE = 128
-TAIL = 8
 
 beta_one = 0.9
 beta_two = 0.95
@@ -37,6 +36,10 @@
 
 def exchange(x, axes):
     return lax.all_to_all(x, axes, split_axis=0, concat_axis=0, tiled=True)
+
+
+def gathered(x, axis):
+    return lax.all_gather(x, axis, axis=0, tiled=True)
 
 
 def turned_column(row):
@@ -61,11 +64,8 @@
         copies[member] = own
 
 
-def spread_body(parts, copies):
-    total = parts[0]
-    for member in range(1, parts.shape[0]):
-        total = total + parts[member]
-    copies[...] = jnp.broadcast_to(total[None], copies.shape)
+def sum_body(parts, out):
+    out[0] = summed(parts)
 
 
 def summed(parts):
@@ -97,7 +97,7 @@
     total = row[:, :SIDE]
     for start in range(SIDE, row.shape[1], SIDE):
         total = total + row[:, start : start + SIDE]
-    lanes[...] = total
+    lanes[0] = total
     factor = root * root * root * stats[blocks:] / D
     for block in range(blocks):
         rows = pl.ds(block * SIDE, SIDE)
@@ -108,36 +108,15 @@
         input_grad[rows, :] = jnp.transpose(grad).astype(BF16)
 
 
-def suffix_body(by_section, top, lanes, payload):
-    sections, block_rows, width = by_section.shape
-    tail = lax.broadcasted_iota(jnp.int32, (TAIL, width), 0)
-    whole = lanes[...]
-    high = whole.astype(BF16).astype(F32)
-    middle = (whole - high).astype(BF16).astype(F32)
-    low = whole - high - middle
-    pieces = jnp.where(tail == 0, high, 0.0)
-    pieces = jnp.where(tail == 1, middle, pieces)
-    pieces = jnp.where(tail == 2, low, pieces).astype(BF16)
+def suffix_body(by_section, top, out):
     running = top[...].astype(F32)
-    for section in range(sections - 1, -1, -1):
+    for section in range(by_section.shape[0] - 1, -1, -1):
         running = running + by_section[section].astype(F32)
-        payload[section, pl.ds(0, block_rows), :] = running.astype(BF16)
-        payload[section, pl.ds(block_rows, TAIL), :] = pieces
-
-
-def square_spread_body(returned, copies):
-    start = returned.shape[1] - TAIL
-    pieces = returned[0, pl.ds(start, TAIL), :].astype(F32)
-    for member in range(1, returned.shape[0]):
-        pieces = pieces + returned[member, pl.ds(start, TAIL), :].astype(F32)
-    lanes = jnp.sum(pieces, axis=0, keepdims=True)
-    copies[...] = jnp.broadcast_to(lanes[None], copies.shape)
-
-
-def leaving_body(returned, out):
-    block_rows = out.shape[1]
-    for owner in range(out.shape[0]):
-        out[owner] = returned[owner, pl.ds(0, block_rows), :]
+        out[section] = running.astype(BF16)
+
+
+def total_body(parts, out):
+    out[...] = jnp.sum(summed(parts), axis=0, keepdims=True)[None]
 
 
 def first_body(key_g, value_g, codes, scale, grads, old, largest):
@@ -163,7 +142,8 @@
 def adam_body(
     parts, grads, first_old, second_old, first_scale, second_scale, largest, way, first, second
 ):
-    total = jnp.sum(summed(parts), axis=1, keepdims=True)
+    total = jnp.sum(summed(parts), axis=0, keepdims=True)
+    total = jnp.sum(total, axis=1, keepdims=True)
     clip_factor = jnp.minimum(1.0, clip_norm / (jnp.sqrt(total) + 1e-06))
     bias_one = 1.0 - beta_one**STEP
     bias_two = 1.0 - beta_two**STEP
@@ -220,41 +200,36 @@
         room=60 * 10**6,
     )(x, norm_gain, keys, values, key_weight[0], value_weight[0])
     parts = exchange(copies, ("shard_1", "shard_2"))
-    copies = kernel_call(
-        spread_body, shape((lax.axis_size("shard_0"), stat_rows, SIDE)), 2**14, 2**17
-    )(parts)
-    parts = exchange(copies, "shard_0")
+    stats = kernel_call(sum_body, shape((1, stat_rows, SIDE)), 2**14, 2**17)(parts)
+    parts = gathered(stats, "shard_0")
 
     key_g, value_g, lanes, input_grad = kernel_call(
         gradient_body,
         (
             shape((width, features)),
             shape((width, features)),
-            shape((1, SIDE)),
+            shape((1, 1, SIDE)),
             shape((row_count, width), BF16),
         ),
         2 * matmul,
         4 * slab,
         scratch_shapes=[pltpu.VMEM((width, row_count), BF16)],
     )(parts, x_turned, u_turned, norm_gain, keys, values)
+    squares = gathered(lanes, "section")
     by_section = exchange(input_grad.reshape(sections, block_rows, width), "section")
-    lanes = lax.psum(lanes, "shard_2")
-    lanes = lax.psum(lanes, "shard_1")
+    squares = gathered(squares.reshape(1, sections, SIDE), "shard_0")
 
     top_rows = lax.dynamic_slice_in_dim(
         top_grad.reshape(row_count, width), lax.axis_index("section") * block_rows, block_rows
     )
-    payload = kernel_call(
-        suffix_body, shape((sections, block_rows + TAIL, width), BF16), slab, slab
-    )(by_section, top_rows, lanes)
-    returned = exchange(payload, "section")
-    copies = kernel_call(
-        square_spread_body, shape((lax.axis_size("shard_0"), 1, SIDE)), 2**14, 2**17
-    )(returned)
-    squares = exchange(copies, "shard_0")
-    leaving = kernel_call(
-        leaving_body, shape((sections, block_rows, width), BF16), slab, slab
-    )(returned).reshape(1, micro_count, token_count, width)
+    suffix = kernel_call(
+        suffix_body, shape((sections, block_rows, width), BF16), slab, slab
+    )(by_section, top_rows)
+    returned = exchange(suffix, "section")
+    leaving = returned.reshape(1, micro_count, token_count, width)
+    lanes = kernel_call(total_body, shape((1, 1, SIDE)), 2**14, 2**17)(squares)
+    squares = gathered(lanes, "shard_1")
+    squares = gathered(squares.reshape(1, lax.axis_size("shard_1"), SIDE), "shard_2")
 
     scale_rows = (2, 1, features)
     first_scales = first_scale.reshape(scale_rows)

time: 103 us -> 139 us (1.35)
  the two profiles are of different devices: /device:TPU:2 before, /device:TPU:1 now
where the time goes in v4:
time: 139 us; the launch traced here: 138 us
  blocking collectives  108 us (78%)
  starting transfers between devices  10.3 us (7%)
  waiting for transfers between devices  8.6 us (6%)
  Pallas kernels  6.96 us (5%)
  local copies, waits for them, and re-layouts  3.03 us (2%)
    all_gather x5, blocking collectives, gathered(): return lax.all_gather(x, axis, axis=0, tiled=True)  86.1 us
    all_to_all x1, blocking collectives, exchange(): return lax.all_to_all(x, axes, split_axis=0, concat_axis=0, tiled=True)  22.3 us
    all_to_all x2, starting transfers between devices, exchange(): return lax.all_to_all(x, axes, split_axis=0, concat_axis=0, tiled=True)  10.3 us
    all_to_all x2, waiting for transfers between devices, exchange(): return lax.all_to_all(x, axes, split_axis=0, concat_axis=0, tiled=True)  8.6 us
    pallas_call x1, Pallas kernels, on_device(): kernel_call(stats_body, (shape((lax.axis_size(('shard_1', 'shard_2')), st...  3.03 us
    unnamed x21, local copies, waits for them, and re-layouts  3.03 us
  transfers between devices with their start and end apart: 2, of which 1 were waited for; matrix products, arithmetic and copies ran while one was open for 0% of the time, Pallas kernels for 2%

profile of v4, /device:TPU:1, one launch (start us, length us, event | category | flops | bytes accessed | tf_op | source)
XLA Modules:
  0.0 138.1 jit_solution(13773317141800626439)
XLA Ops:
  0.6 0.0 copy-start
  0.6 0.0 copy-start.1
  0.7 0.0 copy-start.2
  0.7 3.0 %shard_map.138 = (f32[8,12,128]{2,1,0:T(8,128)}, bf16[128,768]{1,0:T(8,128)(2,1)}, f32[128,768]{1,0:T(8,128)}) custom-call(bf16[768,128]{1,0:T(8,128)(2,1)} %bitcast.31, f32[1,128]{1,0:T(1,128)} %gain.3, bf16[768,512]{1,0:T(8,128)(2,1)} %bitcast.18, bf16[768,512]{1,0:T(8,128)(2,1)} %bitcast.20, bf16[512,128]{1,0:T(8,128)(2,1)} %bitcast.32, ...), custom_call_target="tpu_custom_call" | custom-call | flops 201326592 | bytes 1572864 | tf_op jit(solution)/shard_map/pallas_call | solution.py:191
  3.7 0.0 copy-start.6
  3.7 22.3 %all_to_all.15.parts = f32[8,12,128]{2,1,0:T(8,128)S(1)} all-to-all(f32[8,12,128]{2,1,0:T(8,128)} %get-tuple-element.17), channel_id=1, replica_groups=mesh['section'=8,'shard_0'=16,'shard_1'=4,'shard_2'=2] {'shard_1','shard..., dimensions={0} | all-to-all | bytes 98304 | tf_op jit(solution)/shard_map/all_to_all | solution.py:38
  26.1 24.5 %all_gather.15.parts = f32[16,12,128]{2,1,0:T(8,128)S(1)} all-gather(f32[1,12,128]{2,1,0:T(8,128)S(1)} %shard_map.139), channel_id=1, replica_groups=mesh['section'=8,'shard_0'=16,'shard_1'=4,'shard_2'=2] {'shard_0'}, dimensions={0}, use_global_device_ids=true | all-gather | bytes 104448 | tf_op jit(solution)/shard_map/all_gather | solution.py:42
  50.5 0.0 copy-done.1
  50.5 0.0 copy-done.2
  50.5 0.0 copy-done.6
  50.5 0.6 copy-done.9
  51.2 1.0 copy-done.5
  52.2 1.1 shard_map.140
  53.3 6.8 %all-to-all-start.1 = ((bf16[8,96,128]{2,1,0:T(8,128)(2,1)}), bf16[8,96,128]{2,1,0:T(8,128)(2,1)S(1)}, u32[]{:S(2)}, u32[]{:S(2)}) async-start(bf16[8,96,128]{2,1,0:T(8,128)(2,1)} %bitcast.14), calls=%async_computation.1 | async-start | bytes 393216 | tf_op jit(solution)/shard_map/all_to_all | solution.py:38
  60.1 0.0 copy-done
  60.1 8.6 %all-to-all-done.1.by_section = bf16[8,96,128]{2,1,0:T(8,128)(2,1)S(1)} async-done(((bf16[8,96,128]{2,1,0:T(8,128)(2,1)}), bf16[8,96,128]{2,1,0:T(8,128)(2,1)S(1)}, u32[]{:S(2)}, u32[]{:S(2)}) %all-to-all-start.1) | async-done | bytes 196640 | tf_op jit(solution)/shard_map/all_to_all | solution.py:38
  68.7 0.7 shard_map.145
  69.4 3.5 %all-to-all-start.2 = ((bf16[8,96,128]{2,1,0:T(8,128)(2,1)}), bf16[8,96,128]{2,1,0:T(8,128)(2,1)S(1)}, u32[]{:S(2)}, u32[]{:S(2)}) async-start(bf16[8,96,128]{2,1,0:T(8,128)(2,1)} %shard_map.145), calls=%async_computation.2 | async-start | bytes 393216 | tf_op jit(solution)/shard_map/all_to_all | solution.py:38
  72.9 0.0 copy-done.3
  72.9 0.0 copy-done.8
  72.9 0.0 copy-start.4
  73.0 0.2 shard_map.143.second_old
  73.2 12.4 %all_gather.16 = f32[8,1,128]{2,1,0:T(1,128)S(1)} all-gather(f32[1,1,128]{2,1,0:T(1,128)S(1)} %get-tuple-element.20), channel_id=1, replica_groups=mesh['section'=8,'shard_0'=16,'shard_1'=4,'shard_2'=2] {'section'}, dimensions={0}, use_global_device_ids=true | all-gather | bytes 4608 | tf_op jit(solution)/shard_map/all_gather | solution.py:42
  85.6 20.0 %all-gather = f32[128,1,128]{2,1,0:T(1,128)S(1)} all-gather(f32[8,1,128]{2,1,0:T(1,128)S(1)} %all_gather.16), channel_id=2, replica_groups=mesh['section'=8,'shard_0'=16,'shard_1'=4,'shard_2'=2] {'shard_0'}, dimensions={0}, use_global_device_ids=true | all-gather | bytes 69632 | tf_op jit(solution)/shard_map/all_gather | solution.py:42
  105.6 0.0 copy-done.4
  105.6 0.7 copy-done.7
  106.3 0.3 shard_map.142
  106.6 6.1 %all_gather.18 = f32[4,1,128]{2,1,0:T(1,128)S(1)} all-gather(f32[1,1,128]{2,1,0:T(1,128)S(1)} %shard_map.141), channel_id=1, replica_groups=mesh['section'=8,'shard_0'=16,'shard_1'=4,'shard_2'=2] {'shard_1'}, dimensions={0}, use_global_device_ids=true | all-gather | bytes 2560 | tf_op jit(solution)/shard_map/all_gather | solution.py:42
  112.7 23.1 %all-gather.1 = f32[8,1,128]{2,1,0:T(1,128)S(1)} all-gather(f32[4,1,128]{2,1,0:T(1,128)S(1)} %all_gather.18), channel_id=3, replica_groups=mesh['section'=8,'shard_0'=16,'shard_1'=4,'shard_2'=2] {'shard_2'}, dimensions={0}, use_global_device_ids=true | all-gather | bytes 6144 | tf_op jit(solution)/shard_map/all_gather | solution.py:42
  135.8 1.6 %shard_map.144 = (f32[2,512,128]{2,1,0:T(8,128)}, f32[2,512,128]{2,1,0:T(8,128)}, f32[2,512,128]{2,1,0:T(8,128)}) custom-call(f32[2,4,128]{2,1,0:T(4,128)S(1)} %bitcast.29, f32[2,512,128]{2,1,0:T(8,128)S(1)} %get-tuple-element.23.grads, f32[2,512,128]{2,1,0:T(8,128)S(1)} %get-tuple-element.24.first_old, f32[2,512,128]{2,1,0:T(8,128)S(1)} %shard_map.143.second_old, ...), custom_call_target="tpu_custom_call" | custom-call | flops 10485760 | bytes 3145728 | tf_op jit(solution)/shard_map/pallas_call | solution.py:250
  137.4 0.0 all-to-all-done.2
  137.4 0.7 copy.16
  (8 shorter events, 0.0 us)
Async XLA Ops:
  0.6 59.4 %copy-start = (bf16[2,384,128]{2,1,0:T(8,128)(2,1)S(1)}, bf16[2,384,128]{2,1,0:T(8,128)(2,1)}, u32[]{:S(2)}) copy-start(bf16[2,384,128]{2,1,0:T(8,128)(2,1)} %param.12) | copy-start | bytes 589828
  0.6 49.9 %copy-start.1 = (bf16[1,2,384,512]{3,2,1,0:T(8,128)(2,1)S(1)}, bf16[1,2,384,512]{3,2,1,0:T(8,128)(2,1)}, u32[]{:S(2)}) copy-start(bf16[1,2,384,512]{3,2,1,0:T(8,128)(2,1)} %param.14) | copy-start | bytes 2359300
  0.7 49.9 %copy-start.2 = (bf16[1,2,384,512]{3,2,1,0:T(8,128)(2,1)S(1)}, bf16[1,2,384,512]{3,2,1,0:T(8,128)(2,1)}, u32[]{:S(2)}) copy-start(bf16[1,2,384,512]{3,2,1,0:T(8,128)(2,1)} %param.15) | copy-start | bytes 2359300
  3.7 46.8 %copy-start.6 = (bf16[128,768]{1,0:T(8,128)(2,1)S(1)}, bf16[128,768]{1,0:T(8,128)(2,1)}, u32[]{:S(2)}) copy-start(bf16[128,768]{1,0:T(8,128)(2,1)} %get-tuple-element.18.x_turned) | copy-start | bytes 589828
  50.5 0.7 copy-start.9
  51.2 1.0 copy-start.5
  53.3 15.4 %all-to-all-start.1 = ((bf16[8,96,128]{2,1,0:T(8,128)(2,1)}), bf16[8,96,128]{2,1,0:T(8,128)(2,1)S(1)}, u32[]{:S(2)}, u32[]{:S(2)}) async-start(bf16[8,96,128]{2,1,0:T(8,128)(2,1)} %bitcast.14), calls=%async_computation.1 | async-start | bytes 393216 | tf_op jit(solution)/shard_map/all_to_all | solution.py:38
  60.0 12.9 %copy-start.3 = (s32[1,2,512,128]{3,2,1,0:T(8,128)S(1)}, s32[1,2,512,128]{3,2,1,0:T(8,128)}, u32[]{:S(2)}) copy-start(s32[1,2,512,128]{3,2,1,0:T(8,128)} %param.19) | copy-start | bytes 1572868
  69.4 3.5 %copy-start.8 = (f32[1,2,512,1]{2,3,1,0:T(1,128)S(1)}, f32[1,2,512,1]{2,3,1,0:T(1,128)}, u32[]{:S(2)}) copy-start(f32[1,2,512,1]{2,3,1,0:T(1,128)} %param.21) | copy-start | bytes 12292
  69.4 68.0 %all-to-all-start.2 = ((bf16[8,96,128]{2,1,0:T(8,128)(2,1)}), bf16[8,96,128]{2,1,0:T(8,128)(2,1)S(1)}, u32[]{:S(2)}, u32[]{:S(2)}) async-start(bf16[8,96,128]{2,1,0:T(8,128)(2,1)} %shard_map.145), calls=%async_computation.2 | async-start | bytes 393216 | tf_op jit(solution)/shard_map/all_to_all | solution.py:38
  72.9 32.6 %copy-start.4 = (s32[1,2,512,128]{3,2,1,0:T(8,128)S(1)}, s32[1,2,512,128]{3,2,1,0:T(8,128)}, u32[]{:S(2)}) copy-start(s32[1,2,512,128]{3,2,1,0:T(8,128)} %param.18) | copy-start | bytes 1572868
  105.6 0.7 copy-start.7

commit v5 on v2

--- a/solution.py
+++ b/solution.py
@@ -11,7 +11,7 @@
 STEP = 20
 SHARD = ("shard_0", "shard_1", "shard_2")
 SIDE = 128
-TAIL = 16
+TAIL = 8
 
 beta_one = 0.9
 beta_two = 0.95
@@ -43,7 +43,22 @@
     return jnp.transpose(jnp.broadcast_to(row, (SIDE, SIDE)))
 
 
+def split(row):
+    tail = lax.broadcasted_iota(jnp.int32, (TAIL, row.shape[1]), 0)
+    high = row.astype(BF16).astype(F32)
+    middle = (row - high).astype(BF16).astype(F32)
+    pieces = jnp.where(tail == 0, high, 0.0)
+    pieces = jnp.where(tail == 1, middle, pieces)
+    return jnp.where(tail == 2, row - high - middle, pieces).astype(BF16)
+
+
+def joined(pieces):
+    return jnp.sum(pieces.astype(F32), axis=0, keepdims=True)
+
+
 def stats_body(x, gain, keys, values, key_w, value_w, copies, x_turned, u_turned):
+    width = u_turned.shape[0]
+    x_turned[pl.ds(width, TAIL), pl.ds(0, width)] = split(gain[...])
     gain_column = turned_column(gain[...])
     blocks = x.shape[0] // SIDE
     for block in range(blocks):
@@ -52,7 +67,7 @@
         grad = grad + jnp.dot(values[rows, :], value_w[...], preferred_element_type=F32)
         x_block = jnp.transpose(x[rows, :].astype(F32))
         u_block = gain_column * jnp.transpose(grad)
-        x_turned[:, rows] = x_block.astype(BF16)
+        x_turned[pl.ds(0, width), rows] = x_block.astype(BF16)
         u_turned[:, rows] = u_block
         copies[0, pl.ds(block, 1), :] = jnp.sum(x_block * x_block, axis=0, keepdims=True)
         copies[0, pl.ds(blocks + block, 1), :] = jnp.sum(x_block * u_block, axis=0, keepdims=True)
@@ -61,17 +76,28 @@
         copies[member] = own
 
 
-def spread_body(parts, copies):
-    total = parts[0]
+def spread_body(parts, copies, rows):
+    total = summed(parts)
+    blocks = total.shape[0] // 2
+    power = total[:blocks]
+    high = power.astype(BF16).astype(F32)
+    middle = (power - high).astype(BF16).astype(F32)
+    for piece, value in enumerate((high, middle, power - high - middle, total[blocks:])):
+        rows[pl.ds(piece * blocks, blocks), :] = value
+    copies[...] = jnp.broadcast_to(rows[...].astype(BF16)[None], copies.shape)
+
+
+def power_and_dot(parts):
+    stats = summed(parts)
+    blocks = stats.shape[0] // 4
+    power = stats[:blocks] + stats[blocks : 2 * blocks] + stats[2 * blocks : 3 * blocks]
+    return power, stats[3 * blocks :]
+
+
+def summed(parts):
+    total = parts[0].astype(F32)
     for member in range(1, parts.shape[0]):
-        total = total + parts[member]
-    copies[...] = jnp.broadcast_to(total[None], copies.shape)
-
-
-def summed(parts):
-    total = parts[0]
-    for member in range(1, parts.shape[0]):
-        total = total + parts[member]
+        total = total + parts[member].astype(F32)
     return total
 
 
@@ -80,15 +106,17 @@
 
 
 def gradient_body(
-    parts, x_turned, u_turned, gain, keys, values, key_g, value_g, payload, normed
+    parts, x_turned, u_turned, keys, values, key_g, value_g, payload, normed
 ):
-    stats = summed(parts)
-    blocks = stats.shape[0] // 2
-    root = roots(stats[:blocks])
-    gain_column = turned_column(gain[...])
+    power, row_dot = power_and_dot(parts)
+    blocks = power.shape[0]
+    root = roots(power)
+    features = u_turned.shape[0]
+    own = pl.ds(0, features)
+    gain_column = turned_column(joined(x_turned[pl.ds(features, TAIL), own]))
     for block in range(blocks):
         rows = pl.ds(block * SIDE, SIDE)
-        scaled = x_turned[:, rows].astype(F32) * root[block : block + 1] * gain_column
+        scaled = x_turned[own, rows].astype(F32) * root[block : block + 1] * gain_column
         normed[:, rows] = scaled.astype(BF16)
     key_g[...] = jnp.dot(normed[...], keys[...], preferred_element_type=F32)
     value_g[...] = jnp.dot(normed[...], values[...], preferred_element_type=F32)
@@ -97,14 +125,14 @@
     lanes = row[:, :SIDE]
     for start in range(SIDE, row.shape[1], SIDE):
         lanes = lanes + row[:, start : start + SIDE]
-    factor = root * root * root * stats[blocks:] / D
-    sections, padded_rows, width = payload.shape
+    factor = root * root * root * row_dot / D
+    sections, padded_rows, _ = payload.shape
     block_rows = padded_rows - TAIL
     for block in range(blocks):
         rows = pl.ds(block * SIDE, SIDE)
         grad = (
             u_turned[:, rows] * root[block : block + 1]
-            - x_turned[:, rows].astype(F32) * factor[block : block + 1]
+            - x_turned[own, rows].astype(F32) * factor[block : block + 1]
         )
         grad = jnp.transpose(grad).astype(BF16)
         done = 0
@@ -113,31 +141,25 @@
             count = min(SIDE - done, block_rows - offset)
             payload[section, pl.ds(offset, count), :] = grad[done : done + count]
             done += count
-    tail = lax.broadcasted_iota(jnp.int32, (TAIL, width), 0)
-    high = lanes.astype(BF16).astype(F32)
-    middle = (lanes - high).astype(BF16).astype(F32)
-    low = lanes - high - middle
-    pieces = jnp.where(tail == 0, high, 0.0)
-    pieces = jnp.where(tail == 1, middle, pieces)
-    pieces = jnp.where(tail == 2, low, pieces).astype(BF16)
+    pieces = split(lanes)
     for section in range(sections):
         payload[section, pl.ds(block_rows, TAIL), :] = pieces
 
 
-def square_spread_body(received, copies):
-    start = received.shape[1] - TAIL
-    pieces = received[0, pl.ds(start, TAIL), :].astype(F32)
-    for member in range(1, received.shape[0]):
-        pieces = pieces + received[member, pl.ds(start, TAIL), :].astype(F32)
-    lanes = jnp.sum(pieces, axis=0, keepdims=True)
-    copies[...] = jnp.broadcast_to(lanes[None], copies.shape)
-
-
-def suffix_body(by_section, top, out):
+def suffix_body(received, top, out, lanes):
+    block_rows = top.shape[0]
+    tail = pl.ds(block_rows, TAIL)
     running = top[...].astype(F32)
-    for section in range(by_section.shape[0] - 1, -1, -1):
-        running = running + by_section[section, pl.ds(0, top.shape[0]), :].astype(F32)
+    pieces = jnp.zeros((TAIL, top.shape[1]), F32)
+    for section in range(received.shape[0] - 1, -1, -1):
+        running = running + received[section, pl.ds(0, block_rows), :].astype(F32)
         out[section] = running.astype(BF16)
+        pieces = pieces + received[section, tail, :].astype(F32)
+    lanes[...] = jnp.sum(pieces, axis=0, keepdims=True)
+
+
+def leaving_body(returned, out):
+    out[...] = returned[...]
 
 
 def first_body(key_g, value_g, codes, scale, grads, old, largest):
@@ -212,7 +234,7 @@
         stats_body,
         (
             shape((lax.axis_size(("shard_1", "shard_2")), stat_rows, SIDE)),
-            shape((width, row_count), BF16),
+            shape((width + TAIL, row_count), BF16),
             shape((width, row_count)),
         ),
         2 * matmul,
@@ -221,7 +243,11 @@
     )(x, norm_gain, keys, values, key_weight[0], value_weight[0])
     parts = exchange(copies, ("shard_1", "shard_2"))
     copies = kernel_call(
-        spread_body, shape((lax.axis_size("shard_0"), stat_rows, SIDE)), 2**14, 2**17
+        spread_body,
+        shape((lax.axis_size("shard_0"), 2 * stat_rows, SIDE), BF16),
+        2**14,
+        2**17,
+        scratch_shapes=[pltpu.VMEM((2 * stat_rows, SIDE), F32)],
     )(parts)
     parts = exchange(copies, "shard_0")
 
@@ -235,12 +261,22 @@
         2 * matmul,
         4 * slab,
         scratch_shapes=[pltpu.VMEM((width, row_count), BF16)],
-    )(parts, x_turned, u_turned, norm_gain, keys, values)
+    )(parts, x_turned, u_turned, keys, values)
     received = exchange(payload, "section")
-    copies = kernel_call(
-        square_spread_body, shape((lax.axis_size(SHARD), 1, SIDE)), 2**14, 2**17
-    )(received)
-    squares = exchange(copies, SHARD)
+    top_rows = lax.dynamic_slice_in_dim(
+        top_grad.reshape(row_count, width), lax.axis_index("section") * block_rows, block_rows
+    )
+    suffix, lanes = kernel_call(
+        suffix_body, (shape((sections, block_rows, width), BF16), shape((1, SIDE))), slab, slab
+    )(received, top_rows)
+    returned = exchange(suffix, "section")
+    lanes = lax.psum(lanes, "shard_2")
+    lanes = lax.psum(lanes, "shard_1")
+    copies = jnp.broadcast_to(lanes[None], (lax.axis_size("shard_0"), 1, SIDE))
+    squares = exchange(copies, "shard_0")
+    leaving = kernel_call(
+        leaving_body, shape((row_count, width), BF16), slab, slab
+    )(returned.reshape(row_count, width)).reshape(1, micro_count, token_count, width)
 
     scale_rows = (2, 1, features)
     first_scales = first_scale.reshape(scale_rows)
@@ -254,15 +290,6 @@
     second_old = kernel_call(
         second_body, shape(moments), moment_bytes, 2 * moment_bytes
     )(second_codes[0], second_scales)
-
-    top_rows = lax.dynamic_slice_in_dim(
-        top_grad.reshape(row_count, width), lax.axis_index("section") * block_rows, block_rows
-    )
-    suffix = kernel_call(
-        suffix_body, shape((sections, block_rows, width), BF16), slab, slab
-    )(received, top_rows)
-    returned = exchange(suffix, "section")
-    leaving = returned.reshape(1, micro_count, token_count, width)
 
     whole = pl.BlockSpec(squares.shape, lambda kind: (0, 0, 0))
     one = pl.BlockSpec((1,) + moments[1:], lambda kind: (kind, 0, 0))

time: 103 us -> 107 us (1.039)
  the two profiles are of different devices: /device:TPU:1 before, /device:TPU:2 now
where the time goes in v5:
time: 107 us
  blocking collectives  68.9 us (64%)
  waiting for transfers between devices  16.6 us (16%)
  starting transfers between devices  10.8 us (10%)
  Pallas kernels  7.74 us (7%)
  local copies, waits for them, and re-layouts  1.8 us (2%)
    all_to_all x3, blocking collectives, exchange(): return lax.all_to_all(x, axes, split_axis=0, concat_axis=0, tiled=True)  57.3 us
    all_to_all x2, waiting for transfers between devices, exchange(): return lax.all_to_all(x, axes, split_axis=0, concat_axis=0, tiled=True)  16.6 us
    all_to_all x2, starting transfers between devices, exchange(): return lax.all_to_all(x, axes, split_axis=0, concat_axis=0, tiled=True)  10.8 us
    psum x1, blocking collectives, on_device(): lanes = lax.psum(lanes, 'shard_1')  9.15 us
    pallas_call x1, Pallas kernels, on_device(): kernel_call(stats_body, (shape((lax.axis_size(('shard_1', 'shard_2')), st...  3.02 us
    psum x1, blocking collectives, on_device(): lanes = lax.psum(lanes, 'shard_2')  2.44 us
  transfers between devices with their start and end apart: 2, of which 2 were waited for; matrix products, arithmetic and copies ran while one was open for 0% of the time, Pallas kernels for 2%

profile of v5, /device:TPU:2, one launch (start us, length us, event | category | flops | bytes accessed | tf_op | source)
XLA Modules:
  0.0 106.5 jit_solution(3666865444245791422)
XLA Ops:
  0.6 0.0 copy-start
  0.6 0.0 copy-start.1
  0.7 0.0 copy-start.2
  0.7 3.0 %shard_map.138 = (f32[8,12,128]{2,1,0:T(8,128)}, bf16[136,768]{1,0:T(8,128)(2,1)}, f32[128,768]{1,0:T(8,128)}) custom-call(bf16[768,128]{1,0:T(8,128)(2,1)} %bitcast.28, f32[1,128]{1,0:T(1,128)} %gain.1, bf16[768,512]{1,0:T(8,128)(2,1)} %bitcast.17, bf16[768,512]{1,0:T(8,128)(2,1)} %bitcast.19, bf16[512,128]{1,0:T(8,128)(2,1)} %bitcast.30, ...), custom_call_target="tpu_custom_call" | custom-call | flops 201326592 | bytes 1572864 | tf_op jit(solution)/shard_map/pallas_call | solution.py:233
  3.7 0.0 copy-start.5
  3.7 20.7 %all_to_all.25.parts = f32[8,12,128]{2,1,0:T(8,128)S(1)} all-to-all(f32[8,12,128]{2,1,0:T(8,128)} %get-tuple-element.18), channel_id=1, replica_groups=mesh['section'=8,'shard_0'=16,'shard_1'=4,'shard_2'=2] {'shard_1','shard..., dimensions={0} | all-to-all | bytes 98304 | tf_op jit(solution)/shard_map/all_to_all | solution.py:39
  24.4 20.5 %all_to_all.26.parts = bf16[16,24,128]{2,1,0:T(8,128)(2,1)S(1)} all-to-all(bf16[16,24,128]{2,1,0:T(8,128)(2,1)S(1)} %shard_map.139), channel_id=1, replica_groups=mesh['section'=8,'shard_0'=16,'shard_1'=4,'shard_2'=2] {'shard_0'}, dimensions={0} | all-to-all | bytes 196608 | tf_op jit(solution)/shard_map/all_to_all | solution.py:39
  45.0 0.0 copy-done.1
  45.0 0.0 copy-done.2
  45.0 0.0 copy-done.5
  45.0 0.0 copy-start.6
  45.0 0.9 copy-done.6
  45.9 1.1 %shard_map.140 = (f32[128,512]{1,0:T(8,128)S(1)}, f32[128,512]{1,0:T(8,128)S(1)}, bf16[8,104,128]{2,1,0:T(8,128)(2,1)}) custom-call(bf16[16,24,128]{2,1,0:T(8,128)(2,1)S(1)} %all_to_all.26.parts, bf16[136,768]{1,0:T(8,128)(2,1)S(1)} %copy-done.6, f32[128,768]{1,0:T(8,128)S(1)} %copy-done.5, bf16[768,512]{1,0:T(8,128)(2,1)S(1)} %bitcast.18, ...), custom_call_target="tpu_custom_call" | custom-call | flops 201326592 | bytes 1572864 | tf_op jit(solution)/shard_map/pallas_call | solution.py:254
  47.1 7.2 %all-to-all-start.2 = ((bf16[8,104,128]{2,1,0:T(8,128)(2,1)}), bf16[8,104,128]{2,1,0:T(8,128)(2,1)S(1)}, u32[]{:S(2)}, u32[]{:S(2)}) async-start(bf16[8,104,128]{2,1,0:T(8,128)(2,1)} %get-tuple-element.21), calls=%async_computation.2 | async-start | bytes 425984 | tf_op jit(solution)/shard_map/all_to_all | solution.py:39
  54.3 0.0 copy-done
  54.3 9.9 %all-to-all-done.2.received = bf16[8,104,128]{2,1,0:T(8,128)(2,1)S(1)} async-done(((bf16[8,104,128]{2,1,0:T(8,128)(2,1)}), bf16[8,104,128]{2,1,0:T(8,128)(2,1)S(1)}, u32[]{:S(2)}, u32[]{:S(2)}) %all-to-all-start.2) | async-done | bytes 213024 | tf_op jit(solution)/shard_map/all_to_all | solution.py:39
  64.3 0.7 shard_map.141
  65.0 2.4 %psum.14 = f32[1,128]{1,0:T(1,128)S(1)} all-reduce(f32[1,128]{1,0:T(1,128)S(1)} %get-tuple-element.22), channel_id=1, replica_groups=mesh['section'=8,'shard_0'=16,'shard_1'=4,'shard_2'=2] {'shard_2'}, use_global_device_ids=true, to_apply=%region_0.0 | all-reduce | flops 128 | bytes 1024 | tf_op jit(solution)/shard_map/psum | solution.py:273
  67.4 9.2 %psum.15 = f32[128]{0:T(128)S(1)} all-reduce(f32[128]{0:T(128)S(1)} %bitcast.35), channel_id=1, replica_groups=mesh['section'=8,'shard_0'=16,'shard_1'=4,'shard_2'=2] {'shard_1'}, use_global_device_ids=true, to_apply=%region_1.0 | all-reduce | flops 128 | bytes 1024 | tf_op jit(solution)/shard_map/psum | solution.py:274
  76.6 16.1 %all_to_all.27.parts = f32[16,1,128]{2,1,0:T(1,128)S(1)} all-to-all(f32[16,1,128]{2,1,0:T(1,128)S(1)} %broadcast_in_dim.18), channel_id=1, replica_groups=mesh['section'=8,'shard_0'=16,'shard_1'=4,'shard_2'=2] {'shard_0'}, dimensions={0} | all-to-all | bytes 16384 | tf_op jit(solution)/shard_map/all_to_all | solution.py:39
  92.6 3.5 %all-to-all-start.4 = ((bf16[8,96,128]{2,1,0:T(8,128)(2,1)}), bf16[8,96,128]{2,1,0:T(8,128)(2,1)S(1)}, u32[]{:S(2)}, u32[]{:S(2)}) async-start(bf16[8,96,128]{2,1,0:T(8,128)(2,1)} %get-tuple-element.31), calls=%async_computation.4 | async-start | bytes 393216 | tf_op jit(solution)/shard_map/all_to_all | solution.py:39
  96.2 0.0 copy-done.3
  96.2 0.0 copy-done.8
  96.2 0.0 copy-start.4
  96.2 0.2 shard_map.143.second_old
  96.4 0.0 copy-start.7
  96.4 0.8 copy-done.4
  97.2 0.0 copy-done.7
  97.2 0.3 shard_map.142
  97.6 1.6 %shard_map.144 = (f32[2,512,128]{2,1,0:T(8,128)}, f32[2,512,128]{2,1,0:T(8,128)}, f32[2,512,128]{2,1,0:T(8,128)}) custom-call(f32[16,1,128]{2,1,0:T(1,128)S(1)} %all_to_all.27.parts, f32[2,512,128]{2,1,0:T(8,128)S(1)} %get-tuple-element.25.grads, f32[2,512,128]{2,1,0:T(8,128)S(1)} %get-tuple-element.26.first_old, f32[2,512,128]{2,1,0:T(8,128)S(1)} %shard_map.143.second_old, ...), custom_call_target="tpu_custom_call" | custom-call | flops 10485760 | bytes 3145728 | tf_op jit(solution)/shard_map/pallas_call | solution.py:297
  99.2 6.7 %all-to-all-done.4 = bf16[8,96,128]{2,1,0:T(8,128)(2,1)S(1)} async-done(((bf16[8,96,128]{2,1,0:T(8,128)(2,1)}), bf16[8,96,128]{2,1,0:T(8,128)(2,1)S(1)}, u32[]{:S(2)}, u32[]{:S(2)}) %all-to-all-start.4) | async-done | bytes 196640 | tf_op jit(solution)/shard_map/all_to_all | solution.py:39
  105.8 0.7 shard_map.145
  (5 shorter events, 0.0 us)
Async XLA Ops:
  0.6 53.7 %copy-start = (bf16[2,384,128]{2,1,0:T(8,128)(2,1)S(1)}, bf16[2,384,128]{2,1,0:T(8,128)(2,1)}, u32[]{:S(2)}) copy-start(bf16[2,384,128]{2,1,0:T(8,128)(2,1)} %param.12) | copy-start | bytes 589828
  0.6 44.3 %copy-start.1 = (bf16[1,2,384,512]{3,2,1,0:T(8,128)(2,1)S(1)}, bf16[1,2,384,512]{3,2,1,0:T(8,128)(2,1)}, u32[]{:S(2)}) copy-start(bf16[1,2,384,512]{3,2,1,0:T(8,128)(2,1)} %param.14) | copy-start | bytes 2359300
  0.7 44.3 %copy-start.2 = (bf16[1,2,384,512]{3,2,1,0:T(8,128)(2,1)S(1)}, bf16[1,2,384,512]{3,2,1,0:T(8,128)(2,1)}, u32[]{:S(2)}) copy-start(bf16[1,2,384,512]{3,2,1,0:T(8,128)(2,1)} %param.15) | copy-start | bytes 2359300
  3.7 41.3 %copy-start.5 = (f32[128,768]{1,0:T(8,128)S(1)}, f32[128,768]{1,0:T(8,128)}, u32[]{:S(2)}) copy-start(f32[128,768]{1,0:T(8,128)} %get-tuple-element.20.u_turned) | copy-start | bytes 1179652
  45.0 0.9 copy-start.6
  47.1 49.1 %copy-start.3 = (s32[1,2,512,128]{3,2,1,0:T(8,128)S(1)}, s32[1,2,512,128]{3,2,1,0:T(8,128)}, u32[]{:S(2)}) copy-start(s32[1,2,512,128]{3,2,1,0:T(8,128)} %param.19) | copy-start | bytes 1572868
  47.1 17.2 %all-to-all-start.2 = ((bf16[8,104,128]{2,1,0:T(8,128)(2,1)}), bf16[8,104,128]{2,1,0:T(8,128)(2,1)S(1)}, u32[]{:S(2)}, u32[]{:S(2)}) async-start(bf16[8,104,128]{2,1,0:T(8,128)(2,1)} %get-tuple-element.21), calls=%async_computation.2 | async-start | bytes 425984 | tf_op jit(solution)/shard_map/all_to_all | solution.py:39
  92.6 3.5 %copy-start.8 = (f32[1,2,512,1]{2,3,1,0:T(1,128)S(1)}, f32[1,2,512,1]{2,3,1,0:T(1,128)}, u32[]{:S(2)}) copy-start(f32[1,2,512,1]{2,3,1,0:T(1,128)} %param.21) | copy-start | bytes 12292
  92.6 13.2 %all-to-all-start.4 = ((bf16[8,96,128]{2,1,0:T(8,128)(2,1)}), bf16[8,96,128]{2,1,0:T(8,128)(2,1)S(1)}, u32[]{:S(2)}, u32[]{:S(2)}) async-start(bf16[8,96,128]{2,1,0:T(8,128)(2,1)} %get-tuple-element.31), calls=%async_computation.4 | async-start | bytes 393216 | tf_op jit(solution)/shard_map/all_to_all | solution.py:39
  96.2 1.0 copy-start.4
  96.4 0.8 copy-start.7

commit v6 on v5

--- a/solution.py
+++ b/solution.py
@@ -155,7 +155,7 @@
         running = running + received[section, pl.ds(0, block_rows), :].astype(F32)
         out[section] = running.astype(BF16)
         pieces = pieces + received[section, tail, :].astype(F32)
-    lanes[...] = jnp.sum(pieces, axis=0, keepdims=True)
+    lanes[...] = jnp.broadcast_to(jnp.sum(pieces, axis=0, keepdims=True)[None], lanes.shape)
 
 
 def leaving_body(returned, out):
@@ -267,13 +267,15 @@
         top_grad.reshape(row_count, width), lax.axis_index("section") * block_rows, block_rows
     )
     suffix, lanes = kernel_call(
-        suffix_body, (shape((sections, block_rows, width), BF16), shape((1, SIDE))), slab, slab
+        suffix_body,
+        (shape((sections, block_rows, width), BF16), shape((lax.axis_size("shard_0"), 1, SIDE))),
+        slab,
+        slab,
     )(received, top_rows)
     returned = exchange(suffix, "section")
     lanes = lax.psum(lanes, "shard_2")
     lanes = lax.psum(lanes, "shard_1")
-    copies = jnp.broadcast_to(lanes[None], (lax.axis_size("shard_0"), 1, SIDE))
-    squares = exchange(copies, "shard_0")
+    squares = exchange(lanes, "shard_0")
     leaving = kernel_call(
         leaving_body, shape((row_count, width), BF16), slab, slab
     )(returned.reshape(row_count, width)).reshape(1, micro_count, token_count, width)
@@ -291,15 +293,15 @@
         second_body, shape(moments), moment_bytes, 2 * moment_bytes
     )(second_codes[0], second_scales)
 
-    whole = pl.BlockSpec(squares.shape, lambda kind: (0, 0, 0))
-    one = pl.BlockSpec((1,) + moments[1:], lambda kind: (kind, 0, 0))
-    row = pl.BlockSpec((1,) + scale_rows[1:], lambda kind: (kind, 0, 0))
+    whole = pl.BlockSpec(squares.shape, lambda kind, half: (0, 0, 0))
+    one = pl.BlockSpec((1, features // 2, width), lambda kind, half: (kind, half, 0))
+    row = pl.BlockSpec((1, 1, features // 2), lambda kind, half: (kind, 0, half))
     outputs = kernel_call(
         adam_body,
         (shape(moments),) * 3,
         20 * moment_bytes,
         6 * moment_bytes,
-        grid=(2,),
+        grid=(2, 2),
         in_specs=[whole] + [one] * 3 + [row] * 3,
         out_specs=[one] * 3,
     )(squares, grads, first_old, second_old, first_scales, second_scales, largest)

time: 107 us -> 107 us (level)
  transfers between devices with their start and end apart: 2 -> 2, of which waited for: 2 -> 2; matrix products, arithmetic and copies ran while one was open for 0% -> 0% of each run, Pallas kernels for 2% -> 3%
where the time goes in v6:
time: 107 us
  blocking collectives  69.1 us (65%)
  waiting for transfers between devices  16 us (15%)
  starting transfers between devices  10.8 us (10%)
  Pallas kernels  8.39 us (8%)
  local copies, waits for them, and re-layouts  1.79 us (2%)
    all_to_all x3, blocking collectives, exchange(): return lax.all_to_all(x, axes, split_axis=0, concat_axis=0, tiled=True)  57.3 us
    all_to_all x2, waiting for transfers between devices, exchange(): return lax.all_to_all(x, axes, split_axis=0, concat_axis=0, tiled=True)  16 us
    all_to_all x2, starting transfers between devices, exchange(): return lax.all_to_all(x, axes, split_axis=0, concat_axis=0, tiled=True)  10.8 us
    psum x1, blocking collectives, on_device(): lanes = lax.psum(lanes, 'shard_1')  9.28 us
    pallas_call x1, Pallas kernels, on_device(): kernel_call(stats_body, (shape((lax.axis_size(('shard_1', 'shard_2')), st...  3.02 us
    psum x1, blocking collectives, on_device(): lanes = lax.psum(lanes, 'shard_2')  2.45 us
    pallas_call x1, Pallas kernels, on_device(): kernel_call(adam_body, (shape(moments),) * 3, 20 * moment_bytes, 6 * mome...  2.25 us
  transfers between devices with their start and end apart: 2, of which 2 were waited for; matrix products, arithmetic and copies ran while one was open for 0% of the time, Pallas kernels for 3%

profile of v6, /device:TPU:2, one launch (start us, length us, event | category | flops | bytes accessed | tf_op | source)
XLA Modules:
  0.0 106.7 jit_solution(1979701197000629867)
XLA Ops:
  0.6 0.0 copy-start
  0.6 0.0 copy-start.1
  0.7 0.0 copy-start.2
  0.7 3.0 %shard_map.138 = (f32[8,12,128]{2,1,0:T(8,128)}, bf16[136,768]{1,0:T(8,128)(2,1)}, f32[128,768]{1,0:T(8,128)}) custom-call(bf16[768,128]{1,0:T(8,128)(2,1)} %bitcast.27, f32[1,128]{1,0:T(1,128)} %gain.1, bf16[768,512]{1,0:T(8,128)(2,1)} %bitcast.16, bf16[768,512]{1,0:T(8,128)(2,1)} %bitcast.18, bf16[512,128]{1,0:T(8,128)(2,1)} %bitcast.29, ...), custom_call_target="tpu_custom_call" | custom-call | flops 201326592 | bytes 1572864 | tf_op jit(solution)/shard_map/pallas_call | solution.py:233
  3.7 0.0 copy-start.5
  3.7 20.7 %all_to_all.25.parts = f32[8,12,128]{2,1,0:T(8,128)S(1)} all-to-all(f32[8,12,128]{2,1,0:T(8,128)} %get-tuple-element.18), channel_id=1, replica_groups=mesh['section'=8,'shard_0'=16,'shard_1'=4,'shard_2'=2] {'shard_1','shard..., dimensions={0} | all-to-all | bytes 98304 | tf_op jit(solution)/shard_map/all_to_all | solution.py:39
  24.4 20.5 %all_to_all.26.parts = bf16[16,24,128]{2,1,0:T(8,128)(2,1)S(1)} all-to-all(bf16[16,24,128]{2,1,0:T(8,128)(2,1)S(1)} %shard_map.139), channel_id=1, replica_groups=mesh['section'=8,'shard_0'=16,'shard_1'=4,'shard_2'=2] {'shard_0'}, dimensions={0} | all-to-all | bytes 196608 | tf_op jit(solution)/shard_map/all_to_all | solution.py:39
  45.0 0.0 copy-done.1
  45.0 0.0 copy-done.2
  45.0 0.0 copy-done.5
  45.0 0.0 copy-start.6
  45.0 0.9 copy-done.6
  45.9 1.1 %shard_map.140 = (f32[128,512]{1,0:T(8,128)S(1)}, f32[128,512]{1,0:T(8,128)S(1)}, bf16[8,104,128]{2,1,0:T(8,128)(2,1)}) custom-call(bf16[16,24,128]{2,1,0:T(8,128)(2,1)S(1)} %all_to_all.26.parts, bf16[136,768]{1,0:T(8,128)(2,1)S(1)} %copy-done.6, f32[128,768]{1,0:T(8,128)S(1)} %copy-done.5, bf16[768,512]{1,0:T(8,128)(2,1)S(1)} %bitcast.17, ...), custom_call_target="tpu_custom_call" | custom-call | flops 201326592 | bytes 1572864 | tf_op jit(solution)/shard_map/pallas_call | solution.py:254
  47.1 7.2 %all-to-all-start.2 = ((bf16[8,104,128]{2,1,0:T(8,128)(2,1)}), bf16[8,104,128]{2,1,0:T(8,128)(2,1)S(1)}, u32[]{:S(2)}, u32[]{:S(2)}) async-start(bf16[8,104,128]{2,1,0:T(8,128)(2,1)} %get-tuple-element.21), calls=%async_computation.2 | async-start | bytes 425984 | tf_op jit(solution)/shard_map/all_to_all | solution.py:39
  54.3 0.0 copy-done
  54.3 9.9 %all-to-all-done.2.received = bf16[8,104,128]{2,1,0:T(8,128)(2,1)S(1)} async-done(((bf16[8,104,128]{2,1,0:T(8,128)(2,1)}), bf16[8,104,128]{2,1,0:T(8,128)(2,1)S(1)}, u32[]{:S(2)}, u32[]{:S(2)}) %all-to-all-start.2) | async-done | bytes 213024 | tf_op jit(solution)/shard_map/all_to_all | solution.py:39
  64.3 0.7 shard_map.141
  65.0 2.5 %psum.14 = f32[16,1,128]{2,1,0:T(1,128)S(1)} all-reduce(f32[16,1,128]{2,1,0:T(1,128)S(1)} %get-tuple-element.22), channel_id=1, replica_groups=mesh['section'=8,'shard_0'=16,'shard_1'=4,'shard_2'=2] {'shard_2'}, use_global_device_ids=true, to_apply=%region_0.0 | all-reduce | flops 2048 | bytes 16384 | tf_op jit(solution)/shard_map/psum | solution.py:276
  67.4 9.3 %psum.15 = f32[16,1,128]{2,1,0:T(1,128)S(1)} all-reduce(f32[16,1,128]{2,1,0:T(1,128)S(1)} %psum.14), channel_id=1, replica_groups=mesh['section'=8,'shard_0'=16,'shard_1'=4,'shard_2'=2] {'shard_1'}, use_global_device_ids=true, to_apply=%region_1.0 | all-reduce | flops 2048 | bytes 16384 | tf_op jit(solution)/shard_map/psum | solution.py:277
  76.7 16.1 %all_to_all.27.parts = f32[16,1,128]{2,1,0:T(1,128)S(1)} all-to-all(f32[16,1,128]{2,1,0:T(1,128)S(1)} %psum.15), channel_id=1, replica_groups=mesh['section'=8,'shard_0'=16,'shard_1'=4,'shard_2'=2] {'shard_0'}, dimensions={0} | all-to-all | bytes 16384 | tf_op jit(solution)/shard_map/all_to_all | solution.py:39
  92.8 3.5 %all-to-all-start.4 = ((bf16[8,96,128]{2,1,0:T(8,128)(2,1)}), bf16[8,96,128]{2,1,0:T(8,128)(2,1)S(1)}, u32[]{:S(2)}, u32[]{:S(2)}) async-start(bf16[8,96,128]{2,1,0:T(8,128)(2,1)} %get-tuple-element.31), calls=%async_computation.4 | async-start | bytes 393216 | tf_op jit(solution)/shard_map/all_to_all | solution.py:39
  96.3 0.0 copy-done.3
  96.3 0.0 copy-done.8
  96.3 0.0 copy-start.4
  96.3 0.2 shard_map.143.second_old
  96.5 0.0 copy-start.7
  96.6 0.8 copy-done.4
  97.4 0.0 copy-done.7
  97.4 0.3 shard_map.142
  97.7 2.2 %shard_map.144 = (f32[2,512,128]{2,1,0:T(8,128)}, f32[2,512,128]{2,1,0:T(8,128)}, f32[2,512,128]{2,1,0:T(8,128)}) custom-call(f32[16,1,128]{2,1,0:T(1,128)S(1)} %all_to_all.27.parts, f32[2,512,128]{2,1,0:T(8,128)S(1)} %get-tuple-element.25.grads, f32[2,512,128]{2,1,0:T(8,128)S(1)} %get-tuple-element.26.first_old, f32[2,512,128]{2,1,0:T(8,128)S(1)} %shard_map.143.second_old, ...), custom_call_target="tpu_custom_call" | custom-call | flops 10485760 | bytes 3145728 | tf_op jit(solution)/shard_map/pallas_call | solution.py:299
  100.0 6.0 %all-to-all-done.4 = bf16[8,96,128]{2,1,0:T(8,128)(2,1)S(1)} async-done(((bf16[8,96,128]{2,1,0:T(8,128)(2,1)}), bf16[8,96,128]{2,1,0:T(8,128)(2,1)S(1)}, u32[]{:S(2)}, u32[]{:S(2)}) %all-to-all-start.4) | async-done | bytes 196640 | tf_op jit(solution)/shard_map/all_to_all | solution.py:39
  106.0 0.7 shard_map.145
  (4 shorter events, 0.0 us)
Async XLA Ops:
  0.6 53.7 %copy-start = (bf16[2,384,128]{2,1,0:T(8,128)(2,1)S(1)}, bf16[2,384,128]{2,1,0:T(8,128)(2,1)}, u32[]{:S(2)}) copy-start(bf16[2,384,128]{2,1,0:T(8,128)(2,1)} %param.12) | copy-start | bytes 589828
  0.6 44.3 %copy-start.1 = (bf16[1,2,384,512]{3,2,1,0:T(8,128)(2,1)S(1)}, bf16[1,2,384,512]{3,2,1,0:T(8,128)(2,1)}, u32[]{:S(2)}) copy-start(bf16[1,2,384,512]{3,2,1,0:T(8,128)(2,1)} %param.14) | copy-start | bytes 2359300
  0.7 44.3 %copy-start.2 = (bf16[1,2,384,512]{3,2,1,0:T(8,128)(2,1)S(1)}, bf16[1,2,384,512]{3,2,1,0:T(8,128)(2,1)}, u32[]{:S(2)}) copy-start(bf16[1,2,384,512]{3,2,1,0:T(8,128)(2,1)} %param.15) | copy-start | bytes 2359300
  3.7 41.3 %copy-start.5 = (f32[128,768]{1,0:T(8,128)S(1)}, f32[128,768]{1,0:T(8,128)}, u32[]{:S(2)}) copy-start(f32[128,768]{1,0:T(8,128)} %get-tuple-element.20.u_turned) | copy-start | bytes 1179652
  45.0 0.9 copy-start.6
  47.1 49.2 %copy-start.3 = (s32[1,2,512,128]{3,2,1,0:T(8,128)S(1)}, s32[1,2,512,128]{3,2,1,0:T(8,128)}, u32[]{:S(2)}) copy-start(s32[1,2,512,128]{3,2,1,0:T(8,128)} %param.19) | copy-start | bytes 1572868
  47.1 17.2 %all-to-all-start.2 = ((bf16[8,104,128]{2,1,0:T(8,128)(2,1)}), bf16[8,104,128]{2,1,0:T(8,128)(2,1)S(1)}, u32[]{:S(2)}, u32[]{:S(2)}) async-start(bf16[8,104,128]{2,1,0:T(8,128)(2,1)} %get-tuple-element.21), calls=%async_computation.2 | async-start | bytes 425984 | tf_op jit(solution)/shard_map/all_to_all | solution.py:39
  92.8 3.5 %copy-start.8 = (f32[1,2,512,1]{2,3,1,0:T(1,128)S(1)}, f32[1,2,512,1]{2,3,1,0:T(1,128)}, u32[]{:S(2)}) copy-start(f32[1,2,512,1]{2,3,1,0:T(1,128)} %param.21) | copy-start | bytes 12292
  92.8 13.2 %all-to-all-start.4 = ((bf16[8,96,128]{2,1,0:T(8,128)(2,1)}), bf16[8,96,128]{2,1,0:T(8,128)(2,1)S(1)}, u32[]{:S(2)}, u32[]{:S(2)}) async-start(bf16[8,96,128]{2,1,0:T(8,128)(2,1)} %get-tuple-element.31), calls=%async_computation.4 | async-start | bytes 393216 | tf_op jit(solution)/shard_map/all_to_all | solution.py:39
  96.3 1.0 copy-start.4
  96.5 0.8 copy-start.7
